TPU v7x, 256 devices: a whole 4x4x8 slice. The times are simulated.
256 devices in a mesh: seq: 64 (over z_lo, y, x, core), chan: 4 (over z_hi).
Axes of the slice: x: 4, y: 4, z: 8 (z_hi: 4, z_lo: 2; z = z_hi * 2 + z_lo), core: 2. Of those that a mesh axis runs over, the one named last changes fastest.
Arguments:
- features: bfloat16 [3, 2, 8192, 8192], P(None, None, 'chan', 'seq'), may hold values from -6 to 6
- offsets: int32 [2], replicated, may hold values from 0 to 4095
- tokens: int32 [2, 4], replicated, may hold values from 0 to 511
- decay_rate: float32 [16, 8192], P(None, 'chan'), may hold values from 0 to 1
- residue: float32 [16, 8192], P(None, 'chan'), may hold values from -1 to 1
- skip_weight: float32 [8192], P('chan'), may hold values from -3 to 3
- embedding: bfloat16 [512, 8192], P(None, 'seq'), may hold values from -12 to 12
- norm_gain: float32 [8192], P('seq'), may hold values from 0.1 to 1.9
- dec_weight: bfloat16 [3, 8192, 8192], P(None, 'seq', 'chan'), may hold values from -0.1875 to 0.1875
- out_weight: bfloat16 [8192, 8192], P('chan', 'seq'), may hold values from -0.1875 to 0.1875
Outputs:
- mixed: bfloat16 [2, 8192, 8192], P(None, 'chan', 'seq')
- decoded: bfloat16 [2, 4, 8192], P(None, None, ('seq', 'chan'))
All inputs are finite; a program needn't handle non-finite values.
Results may differ from a plain program's by a relative error of at most 0.0082.
Values may be sent and summed in bfloat16 or wider, within the bound.
No kernel may reach another device: no remote copies, remote signals or barrier semaphores. Data moves between devices by JAX's collectives and lax.ppermute only.
A program may use at most 128 MiB of HBM per device.

v0:
```python
import math

import jax
import jax.numpy as jnp
from jax import lax
from jax.sharding import PartitionSpec as P

D = 8192


highest = lax.Precision.HIGHEST


def local_conv(signal, rates, residues, skips, start_state):
    batch_rows, channels, length = signal.shape
    modes = rates.shape[0]
    block = math.gcd(length, 256)
    blocks = length // block
    group = math.gcd(channels, max(1, 2**21 // (block * block)))
    groups = channels // group

    def one_group(packed):
        sig_group, rate_group, res_group, skip_group, start_group = packed
        expo = -rate_group
        lag_pos = jnp.arange(block, dtype=jnp.float32)
        filt = jnp.sum(res_group[:, :, None] * jnp.exp(expo[:, :, None] * lag_pos), axis=0)
        distance = jnp.arange(block)[:, None] - jnp.arange(block)[None, :]
        toeplitz = jnp.where(distance >= 0, jnp.take(filt, jnp.maximum(distance, 0), axis=1), 0.0)
        blocked = sig_group.reshape(batch_rows, group, blocks, block)
        inner = jnp.einsum("gij,bgnj->bgni", toeplitz, blocked, precision=highest)
        tail_weight = jnp.exp(expo[:, :, None] * (block - 1.0 - lag_pos))
        block_sums = jnp.einsum("mgj,bgnj->bmgn", tail_weight, blocked, precision=highest)
        block_pos = jnp.arange(blocks, dtype=jnp.float32)
        block_gap = block_pos[:, None] - 1.0 - block_pos[None, :]
        spread = jnp.where(
            block_gap >= 0,
            jnp.exp(expo[:, :, None, None] * block * jnp.maximum(block_gap, 0.0)),
            0.0,
        )
        carried = jnp.einsum("mgnk,bmgk->bmgn", spread, block_sums, precision=highest)
        carried = (
            carried + jnp.exp(expo[:, :, None] * block * block_pos)[None] * start_group[..., None]
        )
        head_weight = res_group[:, :, None] * jnp.exp(expo[:, :, None] * (lag_pos + 1.0))
        outer = jnp.einsum("mgi,bmgn->bgni", head_weight, carried, precision=highest)
        conv = (inner + outer).reshape(batch_rows, group, length) + skip_group[
            None, :, None
        ] * sig_group
        final = jnp.exp(expo * block)[None] * carried[..., -1] + block_sums[..., -1]
        return (conv, final)

    packed = (
        signal.reshape(batch_rows, groups, group, length).transpose(1, 0, 2, 3),
        rates.reshape(modes, groups, group).transpose(1, 0, 2),
        residues.reshape(modes, groups, group).transpose(1, 0, 2),
        skips.reshape(groups, group),
        start_state.reshape(batch_rows, modes, groups, group).transpose(2, 0, 1, 3),
    )
    conv, final = lax.map(one_group, packed)
    conv = conv.transpose(1, 0, 2, 3).reshape(batch_rows, channels, length)
    final = final.transpose(1, 2, 0, 3).reshape(batch_rows, modes, channels)
    return (conv, final)


def body(
    features,
    offsets,
    tokens,
    decay_rate,
    residue,
    skip_weight,
    embedding,
    norm_gain,
    dec_weight,
    out_weight,
):
    seq_count = lax.axis_size("seq")
    seq_index = lax.axis_index("seq")
    query = features[0]
    keys_in = features[1]
    values_in = features[2]
    batch_rows, local_chans, shard_len = query.shape
    modes = decay_rate.shape[0]
    positions = seq_index * shard_len + jnp.arange(shard_len, dtype=jnp.int32)
    live = positions[None, :] >= offsets[:, None]
    product = jnp.where(
        live[:, None, :], keys_in.astype(jnp.float32) * values_in.astype(jnp.float32), 0.0
    ).astype(jnp.bfloat16)
    per_device = local_chans // seq_count
    own_rates = lax.dynamic_slice_in_dim(decay_rate, seq_index * per_device, per_device, 1)
    own_residue = lax.dynamic_slice_in_dim(residue, seq_index * per_device, per_device, 1)
    own_skip = lax.dynamic_slice_in_dim(skip_weight, seq_index * per_device, per_device, 0)
    query_part = lax.all_to_all(query, "seq", split_axis=1, concat_axis=2, tiled=True)
    signal_part = lax.all_to_all(product, "seq", split_axis=1, concat_axis=2, tiled=True)
    item_rows = query_part.shape[0]
    start = jnp.zeros((item_rows, modes, per_device), jnp.float32)
    conv, final = local_conv(
        signal_part.astype(jnp.float32), own_rates, own_residue, own_skip, start
    )
    gated = (query_part.astype(jnp.float32) * conv).astype(jnp.bfloat16)
    returned = lax.all_to_all(gated, "seq", split_axis=2, concat_axis=1, tiled=True)
    steps = tokens.shape[1]
    vocab = embedding.shape[0]
    flat_tokens = tokens.reshape(-1)
    one_hot = (flat_tokens[:, None] == jnp.arange(vocab, dtype=jnp.int32)[None, :]).astype(
        jnp.bfloat16
    )
    embedded = jnp.dot(one_hot, embedding, preferred_element_type=jnp.float32)
    partial_sq = jnp.sum(embedded * embedded, axis=1)
    total_sq = lax.psum(partial_sq, "seq")
    normed = (embedded * lax.rsqrt(total_sq / D + 1e-05)[:, None] * norm_gain[None, :]).astype(
        jnp.bfloat16
    )
    proj_terms = jnp.einsum("td,idc->itc", normed, dec_weight, preferred_element_type=jnp.float32)
    projected = lax.psum_scatter(proj_terms, "seq", scatter_dimension=2, tiled=True).astype(
        jnp.bfloat16
    )
    projected = projected.reshape(3, batch_rows, steps, per_device)
    decay = jnp.exp(-own_rates)
    running = final
    outputs = []
    for step in range(steps):
        rounded = lax.optimization_barrier(
            (
                projected[1, :, step].astype(jnp.float32)
                * projected[2, :, step].astype(jnp.float32)
            ).astype(jnp.bfloat16)
        )
        mixed_in = rounded.astype(jnp.float32)
        running = decay[None] * running + mixed_in[:, None, :]
        conv_step = jnp.sum(own_residue[None] * running, axis=1) + own_skip[None] * mixed_in
        outputs.append((projected[0, :, step].astype(jnp.float32) * conv_step).astype(jnp.bfloat16))
    decode_mix = jnp.stack(outputs, axis=1)
    piece = lax.all_gather(decode_mix, "seq", axis=2, tiled=True)
    piece_width = piece.shape[2]
    summed = jnp.dot(piece.reshape(-1, piece_width), out_weight, preferred_element_type=jnp.float32)
    decoded = lax.psum_scatter(summed, "chan", scatter_dimension=1, tiled=True).astype(jnp.bfloat16)
    decoded = decoded.reshape(batch_rows, steps, -1)
    return (returned, decoded)


def solution(mesh):
    placed = (
        P(None, None, "chan", "seq"),
        P(),
        P(),
        P(None, "chan"),
        P(None, "chan"),
        P("chan"),
        P(None, "seq"),
        P("seq"),
        P(None, "seq", "chan"),
        P("chan", "seq"),
    )
    return jax.shard_map(
        body,
        mesh=mesh,
        in_specs=placed,
        out_specs=(P(None, "chan", "seq"), P(None, None, ("seq", "chan"))),
        check_vma=False,
    )
```

profile of v0, /device:TPU:1, one launch (start us, length us, event | category | flops | bytes accessed | tf_op | source)
XLA Modules:
  0.0 973.6 jit_solution(962015850110151932)
XLA Ops:
  7.2 3.5 fusion.69
  11.5 13.2 %fusion.19 = bf16[2,2048,128]{2,0,1:T(2,128)(2,1)} fusion(pred[2,128]{1,0:T(4,128)(4,1)S(1)} %broadcast_compare_fusion, bf16[1,2,2048,128]{3,2,1,0:T(8,128)(2,1)} %get-tuple-element.31, bf16[1,2,2048,128]{3,2,1,0:T(8,128)(2,1)S(1)} %get-tuple-element.30), kind=kLoop, calls=%fused_computation.24 | loop fusion | flops 2621440 | bytes 3145984 | tf_op jit(solution)/shard_map/convert_element_type | solution.py:88
  24.7 10.3 %all-to-all-start.1 = ((bf16[2,2048,128]{2,0,1:T(2,128)(2,1)}), bf16[2,2048,128]{2,0,1:T(2,128)(2,1)S(1)}, u32[]{:S(2)}, u32[]{:S(2)}) async-start(bf16[2,2048,128]{2,0,1:T(2,128)(2,1)} %fusion.19), calls=%async_computation.1 | async-start | bytes 2097152 | tf_op jit(solution)/shard_map/all_to_all | solution.py:94
  37.0 3.6 copy.213
  40.8 11.2 %all-to-all-done.1 = bf16[2,2048,128]{2,0,1:T(2,128)(2,1)S(1)} async-done(((bf16[2,2048,128]{2,0,1:T(2,128)(2,1)}), bf16[2,2048,128]{2,0,1:T(2,128)(2,1)S(1)}, u32[]{:S(2)}, u32[]{:S(2)}) %all-to-all-start.1) | async-done | bytes 1048608 | tf_op jit(solution)/shard_map/all_to_all | solution.py:94
  52.0 5.3 all-to-all-start
  57.4 147.1 %psum.7 = f32[8]{0:T(128)S(1)} all-reduce(f32[8]{0:T(128)S(1)} %get-tuple-element.52), channel_id=1, replica_groups=mesh['seq'=64,'chan'=4] {'seq'}, use_global_device_ids=true, to_apply=%region_2.3 | all-reduce | flops 8 | bytes 64 | tf_op jit(solution)/shard_map/psum | solution.py:110
  205.3 217.0 %gather_fusion = f32[65536,32]{1,0:T(8,128)} fusion(f32[32,256]{0,1:T(8,128)S(1)} %copy.128, s32[65536]{0:T(1024)S(1)} %broadcast_clamp_fusion), kind=kCustom, calls=%fused_computation | custom fusion | bytes 17039360 | tf_op jit(solution)/shard_map/while/body/eval_jaxpr/jit(_take)/gather | solution.py:28
  422.4 22.2 %copy.129 = f32[256,256,32]{1,0,2:T(8,128)} copy(f32[256,256,32]{2,1,0:T(8,128)} %bitcast.138) | data formatting | bytes 16777216 | tf_op jit(solution)/shard_map/while/body/eval_jaxpr/jit(_take)/gather | solution.py:28
  451.3 13.7 %fusion.23 = f32[2,16,32,32]{3,0,2,1:T(2,128)S(1)} fusion(f32[32,32]{1,0:T(8,128)S(1)} %fusion.43, f32[16,32]{1,0:T(8,128)S(1)} %get-tuple-element.35, pred[32,32]{1,0:T(8,128)(4,1)S(1)} %fusion.44, f32[2,16,32,32]{3,1,0,2:T(8,128)S(1)} %convolution_bitcast_fusion.1, f32[16,32,32]{2,1,0:T(8,128)S(1)} %exponential_multiply_fusion), kind=kOutput, calls=%fused_computation.28 | convolution fusion | flops 13664256 | bytes 334848 | tf_op jit(solution)/shard_map/while/body/eval_jaxpr/mgnk,bmgk->bmgn/dot_general | solution.py:40
  465.0 8.7 fusion
  473.8 3.8 add_bitcast_fusion
  477.6 7.8 copy.154
  485.4 7.8 copy.132
  496.7 11.7 %copy.122 = f32[2,32,64,128]{1,0,3,2:T(2,128)} copy(f32[2,32,64,128]{3,0,1,2:T(2,128)} %convert_bitcast_fusion) | data formatting | bytes 4194304 | tf_op jit(solution)/shard_map/convert_element_type | solution.py:100
  508.4 11.1 %fusion.4 = bf16[2,32,8192]{1,0,2:T(2,128)(2,1)} fusion(f32[2,32,64,128]{1,0,3,2:T(2,128)} %copy.132, f32[2,32,32,256]{1,0,3,2:T(2,128)} %copy.154, f32[2,32,64,128]{1,0,3,2:T(2,128)} %copy.122, f32[32]{0:T(128)S(1)} %dynamic_slice.25), kind=kLoop, calls=%fused_computation.6 | loop fusion | flops 2097152 | bytes 7340160 | tf_op jit(solution)/shard_map/convert_element_type | solution.py:100
  519.5 10.1 %reshape.228 = bf16[64,2,4096]{2,1,0:T(2,128)(2,1)} reshape(bf16[8192,2,32]{2,1,0:T(2,128)(2,1)} %bitcast.141) | data formatting | bytes 2097152
  529.6 5.1 all-to-all-start.2
  538.2 5.2 reshape.224
  543.5 288.1 %reduce-scatter.7.cloned.1.call-done = f32[32,24]{1,0:T(8,128)} async-done(((f32[2048,24]{1,0:T(8,128)}), f32[32,24]{1,0:T(8,128)}) %reduce-scatter.7.cloned.1.call-update) | async-done | bytes 3088
  838.1 90.1 %all_gather.3 = bf16[2,4,2048]{1,0,2:T(2,128)(2,1)} all-gather(bf16[2,4,32]{1,0,2:T(2,128)(2,1)S(1)} %copy.149), channel_id=1, replica_groups=mesh['seq'=64,'chan'=4] {'seq'}, dimensions={2}, use_global_device_ids=true | all-gather | bytes 33280 | tf_op jit(solution)/shard_map/all_gather | solution.py:134
  932.9 19.6 %reduce-scatter.9.cloned.1.call-done = f32[32,8]{1,0:T(8,128)} async-done(((f32[128,8]{1,0:T(8,128)}), f32[32,8]{1,0:T(8,128)}) %reduce-scatter.9.cloned.1.call-update) | async-done | bytes 1040
  953.8 3.5 reshape.229
  957.3 9.0 copy.134
  (67 shorter events, 29.8 us)
Async XLA Ops:
  7.2 527.6 %copy-start = (bf16[3,128,2048]{2,1,0:T(8,128)(2,1)S(1)}, bf16[3,128,2048]{2,1,0:T(8,128)(2,1)}, u32[]{:S(2)}) copy-start(bf16[3,128,2048]{2,1,0:T(8,128)(2,1)} %param.18) | copy-start | bytes 4718596
  7.2 28.9 %copy-start.5 = (s32[2,4]{1,0:T(2,128)S(1)}, s32[2,4]{1,0:T(2,128)}, u32[]{:S(2)}) copy-start(s32[2,4]{1,0:T(2,128)} %param.12) | copy-start | bytes 100
  7.2 29.1 %copy-start.4 = (bf16[512,128]{1,0:T(8,128)(2,1)S(1)}, bf16[512,128]{1,0:T(8,128)(2,1)}, u32[]{:S(2)}) copy-start(bf16[512,128]{1,0:T(8,128)(2,1)} %param.16) | copy-start | bytes 393220
  24.7 27.4 %all-to-all-start.1 = ((bf16[2,2048,128]{2,0,1:T(2,128)(2,1)}), bf16[2,2048,128]{2,0,1:T(2,128)(2,1)S(1)}, u32[]{:S(2)}, u32[]{:S(2)}) async-start(bf16[2,2048,128]{2,0,1:T(2,128)(2,1)} %fusion.19), calls=%async_computation.1 | async-start | bytes 2097152 | tf_op jit(solution)/shard_map/all_to_all | solution.py:94
  52.0 441.2 %all-to-all-start = ((bf16[2,2048,128]{2,0,1:T(2,128)(2,1)}), bf16[2,2048,128]{2,0,1:T(2,128)(2,1)}, u32[]{:S(2)}, u32[]{:S(2)}) async-start(bf16[2,2048,128]{2,0,1:T(2,128)(2,1)} %bitcast.137), calls=%async_computation | async-start | bytes 2097152 | tf_op jit(solution)/shard_map/all_to_all | solution.py:93
  451.3 13.7 %copy-start.1 = (f32[2,16,32,32]{3,1,0,2:T(8,128)}, f32[2,16,32,32]{3,1,0,2:T(8,128)S(1)}, u32[]{:S(2)}) copy-start(f32[2,16,32,32]{3,1,0,2:T(8,128)S(1)} %convolution_bitcast_fusion.1) | copy-start | bytes 393220
  465.0 8.7 copy-start.2
  508.4 26.4 %copy-start.3 = (f32[128]{0:T(128)S(1)}, f32[128]{0:T(128)}, u32[]{:S(2)}) copy-start(f32[128]{0:T(128)} %param.17) | copy-start | bytes 1540
  529.6 424.2 %all-to-all-start.2 = ((bf16[64,2,4096]{2,1,0:T(2,128)(2,1)}), bf16[64,2,4096]{2,1,0:T(2,128)(2,1)S(1)}, u32[]{:S(2)}, u32[]{:S(2)}) async-start(bf16[64,2,4096]{2,1,0:T(2,128)(2,1)} %reshape.228), calls=%async_computation.2 | async-start | bytes 2097152 | tf_op jit(solution)/shard_map/all_to_all | solution.py:101
  534.7 296.9 %reduce-scatter.7.cloned.1.call-start = ((), (), s32[]{:S(2)}) async-start(), calls=%async_computation.5 | async-start | bytes 1064960
  543.4 409.0 %reduce-scatter.9.cloned.1.call-start = ((), (), s32[]{:S(2)}) async-start(), calls=%async_computation.6 | async-start | bytes 81920
Sparse Core Ops, SparseCore 0:
  543.5 288.0 reduce-scatter.6
  933.0 19.4 reduce-scatter.8
where the time goes:
time: 986 us; the launch traced here: 974 us
  waiting for transfers between devices  319 us (32%)
  local copies, waits for them, and re-layouts  318 us (32%)
  blocking collectives  237 us (24%)
  other arithmetic  33 us (3%)
  matrix products  31.1 us (3%)
  starting transfers between devices  20.8 us (2%)
  between operations  14.8 us (2%)
    unnamed x4, waiting for transfers between devices  308 us
    gather x2, local copies, waits for them, and re-layouts, one_group(): jnp.take(filt, jnp.maximum(distance, 0), axis=1)  239 us
    psum x1, blocking collectives, body(): total_sq = lax.psum(partial_sq, 'seq')  147 us
    all_gather x1, blocking collectives, body(): piece = lax.all_gather(decode_mix, 'seq', axis=2, tiled=True)  90.1 us
    unnamed x21, local copies, waits for them, and re-layouts  27.9 us
  transfers between devices with their start and end apart: 5, of which 3 were waited for; matrix products, arithmetic and copies ran while one was open for 32% of the time, Pallas kernels for 0%

commit v1 on v0

v1 whole, which is shorter than its diff:
```python
import jax
import jax.numpy as jnp
from jax import lax
from jax.experimental import pallas as pl
from jax.experimental.pallas import tpu as pltpu
from jax.sharding import PartitionSpec as P

LANES = 128
SUB = 8
EPS = 1e-05


def quarter_of(shape):
    return lax.broadcasted_iota(jnp.int32, shape, len(shape) - 1) // 32


def spread(tiles, sign):
    quarter = quarter_of((SUB, LANES))
    made = []
    for q in range(4):
        total = None
        for r in range(4):
            shift = (32 * (r - q)) % LANES
            moved = tiles[r] if shift == 0 else pltpu.roll(tiles[r], shift, 1)
            total = moved if total is None else jnp.where(quarter == r, moved, total)
        made.append(total)
    return made


def rounded(x):
    return x.astype(jnp.bfloat16).astype(jnp.float32)


def first_kernel(modes, shard, tokens, offsets, k_ref, v_ref, rate_ref, emb_ref, gain_ref, w_ref,
                 u_out, send, trans, decay, state, x16, squares):
    half = pl.program_id(0)
    position = lax.axis_index("seq") * shard + lax.broadcasted_iota(jnp.int32, (LANES, shard), 1)
    batch = k_ref.shape[1]
    steps = tokens.shape[1]
    count = batch * steps

    @pl.when(half == 0)
    def _():
        vocab = emb_ref.shape[0]
        row = lax.broadcasted_iota(jnp.int32, (16, vocab), 0)
        wanted = jnp.full((16, vocab), -1, jnp.int32)
        for t in range(count):
            wanted = jnp.where(row == t, tokens[t // steps, t % steps], wanted)
        hot = (lax.broadcasted_iota(jnp.int32, (16, vocab), 1) == wanted).astype(jnp.float32)
        x = jnp.dot(hot.astype(jnp.bfloat16), emb_ref[...], preferred_element_type=jnp.float32)[:SUB]
        squares[...] = jnp.broadcast_to(jnp.sum(x * x, axis=1, keepdims=True), (SUB, LANES))
        scaled = x * gain_ref[...]
        high = rounded(scaled)
        x16[...] = jnp.concatenate([high, scaled - high], axis=0).astype(jnp.bfloat16)

    for g in range(SUB):
        decay[pl.ds(g, modes, stride=SUB), :] = jnp.exp(-rate_ref[:, g * LANES:(g + 1) * LANES])
        for b in range(batch):
            rows = slice(g * LANES, (g + 1) * LANES)
            product = k_ref[0, b, rows].astype(jnp.float32) * v_ref[0, b, rows].astype(jnp.float32)
            u = rounded(jnp.where(position >= offsets[b], product, 0.0))
            trans[pl.ds((b * SUB + g) * shard, shard), :] = u.T

    rates = [decay[m * SUB:(m + 1) * SUB, :] for m in range(modes)]

    def step(t, held):
        held = list(held)
        for b in range(batch):
            u = trans[pl.ds(b * SUB * shard + t, SUB, stride=shard), :]
            u_out[0, b, t] = u
            for m in range(modes):
                at = b * modes + m
                held[at] = rates[m] * held[at] + u
        return tuple(held)

    zero = jnp.zeros((SUB, LANES), jnp.float32)
    held = lax.fori_loop(0, shard, step, (zero,) * (batch * modes), unroll=2)
    for at in range(batch * modes):
        state[at * SUB:(at + 1) * SUB, :] = held[at]

    terms = []
    for i in range(3):
        both = jnp.dot(x16[...], w_ref[i], preferred_element_type=jnp.float32)
        terms.append(both[:SUB] + both[SUB:])
    for g in range(SUB):
        ends = spread([state[pl.ds(g + r * 64, SUB, stride=SUB), :] for r in range(4)], 1)
        parts = spread([t[:, g * LANES:(g + 1) * LANES] for t in terms] + [squares[...]], 1)
        for q in range(4):
            send[g * 4 + q, :SUB] = ends[q]
            send[g * 4 + q, SUB:] = parts[q]


def owner_kernel(width, shard, steps, got, rate_ref, res_ref, skip_ref, back):
    owner = lax.axis_index("seq")
    group, part = owner // 4, owner % 4
    turn = (LANES - 32 * part) % LANES
    quarter = quarter_of((SUB, LANES))

    def four(a, b, c, d):
        b, c, d = pltpu.roll(b, 32, 1), pltpu.roll(c, 64, 1), pltpu.roll(d, 96, 1)
        return jnp.where(quarter == 0, a, jnp.where(quarter == 1, b, jnp.where(quarter == 2, c, d)))

    def packed(ref):
        own = ref[:, pl.ds(pl.multiple_of(group * LANES, LANES), LANES)]
        own = pltpu.roll(own, turn, 1)
        low, high = own[:SUB], own[SUB:]
        return four(low, high, low, high)

    rate = packed(rate_ref)
    res = packed(res_ref)
    jump = jnp.exp(-rate * shard)
    carried = jnp.zeros((SUB, LANES), jnp.float32)
    total = jnp.zeros((SUB, LANES), jnp.float32)
    for i in range(got.shape[0]):
        back[i, :SUB] = carried
        carried = jump * carried + got[i, :SUB]
        total = total + got[i, SUB:]
    scale = lax.rsqrt(pltpu.roll(total, 32, 1) / width + EPS)
    query = rounded(total * scale)
    key = rounded(pltpu.roll(total, 96, 1) * scale)
    value = rounded(pltpu.roll(total, 64, 1) * scale)
    weight = rounded(key * value)
    weight = four(weight, weight, weight, weight)
    skip = jnp.broadcast_to(skip_ref[pl.ds(group, 1), :], (SUB, LANES))
    skip = pltpu.roll(skip, turn, 1)
    skip = four(skip, skip, skip, skip)
    decay = jnp.exp(-rate)
    row = lax.broadcasted_iota(jnp.int32, (SUB, LANES), 0)
    conv = jnp.zeros((SUB, LANES), jnp.float32)
    for s in range(steps):
        first = jnp.broadcast_to(weight[s:s + 1], (SUB, LANES))
        second = jnp.broadcast_to(weight[steps + s:steps + s + 1], (SUB, LANES))
        w = jnp.where(quarter < 2, first, second)
        carried = decay * carried + w
        summed = jnp.broadcast_to(jnp.sum(res * carried, axis=0, keepdims=True), (SUB, LANES))
        summed = summed + pltpu.roll(summed, 96, 1) + skip * w
        conv = jnp.where(row == s, summed, conv)
        conv = jnp.where(row == steps + s, pltpu.roll(summed, 64, 1), conv)
    mix = rounded(query * conv)
    for i in range(got.shape[0]):
        back[i, SUB:] = mix


def decode_kernel(mix_ref, w_ref, out):
    quarter = quarter_of((SUB, LANES))
    pieces = []
    for g in range(mix_ref.shape[0] // 4):
        tile = mix_ref[g * 4]
        for q in range(1, 4):
            tile = jnp.where(quarter == q, pltpu.roll(mix_ref[g * 4 + q], 32 * q, 1), tile)
        pieces.append(tile)
    mix = jnp.concatenate(pieces, axis=1).astype(jnp.bfloat16)
    summed = jnp.dot(mix, w_ref[...], preferred_element_type=jnp.float32)
    for k in range(4):
        out[k] = summed[:, k * 32:(k + 1) * 32]


def last_kernel(modes, shard, carry_ref, u_ref, q_ref, rate_ref, res_ref, skip_ref,
                out, trans, decay, weight, state):
    batch = u_ref.shape[1]
    for g in range(SUB):
        lanes = slice(g * LANES, (g + 1) * LANES)
        decay[pl.ds(g, modes, stride=SUB), :] = jnp.exp(-rate_ref[:, lanes])
        weight[pl.ds(g, modes, stride=SUB), :] = res_ref[:, lanes]
        tiles = spread([carry_ref[g * 4 + q] for q in range(4)], 1)
        for r in range(4):
            state[pl.ds(g + r * 64, SUB, stride=SUB), :] = tiles[r]
    rates = [decay[m * SUB:(m + 1) * SUB, :] for m in range(modes)]
    weights = [weight[m * SUB:(m + 1) * SUB, :] for m in range(modes)]
    skip = skip_ref[...]
    for b in range(batch):
        def step(t, held):
            held = list(held)
            u = u_ref[0, b, t]
            terms = [skip * u]
            for m in range(modes):
                held[m] = rates[m] * held[m] + u
                terms.append(weights[m] * held[m])
            while len(terms) > 1:
                terms = [x + y for x, y in zip(terms[::2], terms[1::2])] + terms[len(terms) // 2 * 2:]
            trans[pl.ds(t, SUB, stride=shard), :] = terms[0]
            return tuple(held)

        held = tuple(state[(b * modes + m) * SUB:(b * modes + m + 1) * SUB, :] for m in range(modes))
        lax.fori_loop(0, shard, step, held, unroll=2)
        for g in range(SUB):
            rows = slice(g * LANES, (g + 1) * LANES)
            conv = trans[pl.ds(g * shard, shard), :].T
            out[b, rows] = (q_ref[0, b, rows].astype(jnp.float32) * conv).astype(jnp.bfloat16)


def body(features, offsets, tokens, decay_rate, residue, skip_weight, embedding, norm_gain, dec_weight, out_weight):
    _, batch, chans, shard = features.shape
    modes = decay_rate.shape[0]
    steps = tokens.shape[1]
    vocab = embedding.shape[0]
    devices = lax.axis_size("seq")
    width = devices * norm_gain.shape[0]
    block = SUB * LANES
    halves = chans // block
    f32 = jnp.float32
    gain = norm_gain.reshape(1, -1)
    skip = skip_weight.reshape(chans // LANES, LANES)

    u_t, send = pl.pallas_call(
        lambda *refs: first_kernel(modes, shard, *refs),
        grid_spec=pltpu.PrefetchScalarGridSpec(
            num_scalar_prefetch=2,
            grid=(halves,),
            in_specs=[
                pl.BlockSpec((1, batch, block, shard), lambda h, *_: (1, 0, h, 0)),
                pl.BlockSpec((1, batch, block, shard), lambda h, *_: (2, 0, h, 0)),
                pl.BlockSpec((modes, block), lambda h, *_: (0, h)),
                pl.BlockSpec((vocab, shard), lambda h, *_: (0, 0)),
                pl.BlockSpec((1, shard), lambda h, *_: (0, 0)),
                pl.BlockSpec((3, shard, block), lambda h, *_: (0, 0, h)),
            ],
            out_specs=[
                pl.BlockSpec((1, batch, shard, SUB, LANES), lambda h, *_: (h, 0, 0, 0, 0)),
                pl.BlockSpec((devices // halves, 2 * SUB, LANES), lambda h, *_: (h, 0, 0)),
            ],
            scratch_shapes=[
                pltpu.VMEM((batch * SUB * shard, LANES), f32),
                pltpu.VMEM((modes * SUB, LANES), f32),
                pltpu.VMEM((batch * modes * SUB, LANES), f32),
                pltpu.VMEM((16, shard), jnp.bfloat16),
                pltpu.VMEM((SUB, LANES), f32),
            ],
        ),
        out_shape=[
            jax.ShapeDtypeStruct((halves, batch, shard, SUB, LANES), f32),
            jax.ShapeDtypeStruct((devices, 2 * SUB, LANES), f32),
        ],
        name="first",
    )(tokens, offsets, features, features, decay_rate, embedding, gain, dec_weight)

    got = lax.all_to_all(send, "seq", split_axis=0, concat_axis=0, tiled=True)

    back = pl.pallas_call(
        lambda *refs: owner_kernel(width, shard, steps, *refs),
        out_shape=jax.ShapeDtypeStruct((devices, 2 * SUB, LANES), f32),
        name="owner",
    )(got, decay_rate, residue, skip)

    given = lax.all_to_all(back, "seq", split_axis=0, concat_axis=0, tiled=True)

    partial = pl.pallas_call(
        decode_kernel,
        grid=(1,),
        in_specs=[
            pl.BlockSpec((devices, SUB, LANES), lambda i: (0, 1, 0)),
            pl.BlockSpec((chans, LANES), lambda i: (0, 0)),
        ],
        out_specs=pl.BlockSpec((4, SUB, 32), lambda i: (0, 0, 0)),
        out_shape=jax.ShapeDtypeStruct((4, SUB, 32), f32),
        name="decode",
    )(given, out_weight)
    pieces = lax.all_to_all(partial, "chan", split_axis=0, concat_axis=0, tiled=True)
    decoded = jnp.sum(pieces, axis=0).astype(jnp.bfloat16).reshape(batch, steps, 32)

    mixed = pl.pallas_call(
        lambda *refs: last_kernel(modes, shard, *refs),
        grid=(halves,),
        in_specs=[
            pl.BlockSpec((devices // halves, SUB, LANES), lambda h: (h, 0, 0)),
            pl.BlockSpec((1, batch, shard, SUB, LANES), lambda h: (h, 0, 0, 0, 0)),
            pl.BlockSpec((1, batch, block, shard), lambda h: (0, 0, h, 0)),
            pl.BlockSpec((modes, block), lambda h: (0, h)),
            pl.BlockSpec((modes, block), lambda h: (0, h)),
            pl.BlockSpec((SUB, LANES), lambda h: (h, 0)),
        ],
        out_specs=pl.BlockSpec((batch, block, shard), lambda h: (0, h, 0)),
        out_shape=jax.ShapeDtypeStruct((batch, chans, shard), jnp.bfloat16),
        scratch_shapes=[
            pltpu.VMEM((SUB * shard, LANES), f32),
            pltpu.VMEM((modes * SUB, LANES), f32),
            pltpu.VMEM((modes * SUB, LANES), f32),
            pltpu.VMEM((batch * modes * SUB, LANES), f32),
        ],
        cost_estimate=pl.CostEstimate(flops=2**25, bytes_accessed=2**22, transcendentals=0),
        name="last",
    )(given, u_t, features, decay_rate, residue, skip)
    return (mixed, decoded)


def solution(mesh):
    placed = (
        P(None, None, "chan", "seq"),
        P(),
        P(),
        P(None, "chan"),
        P(None, "chan"),
        P("chan"),
        P(None, "seq"),
        P("seq"),
        P(None, "seq", "chan"),
        P("chan", "seq"),
    )
    return jax.shard_map(
        body,
        mesh=mesh,
        in_specs=placed,
        out_specs=(P(None, "chan", "seq"), P(None, None, ("seq", "chan"))),
        check_vma=False,
    )
```

time: 986 us -> 74.9 us (0.08); the launches traced: 974 us -> 74.5 us
  waiting for transfers between devices: 319 us -> 0.01 us
  local copies, waits for them, and re-layouts: 318 us -> 1.97 us
  blocking collectives: 237 us -> 39.9 us
  other arithmetic: 33 us -> 1.25 us
  matrix products: 31.1 us -> 0 us
  Pallas kernels: 0 us -> 23.4 us
  between operations: 14.8 us -> 0.64 us
  starting transfers between devices: 20.8 us -> 7.28 us
    unnamed x4 -> x0, waiting for transfers between devices: 308 us -> none
    gather x2 -> x0, local copies, waits for them, and re-layouts: 239 us -> none  [one_group(): jnp.take(filt, jnp.maximum(distance, 0), axis=1)]
    psum x1 -> x0, blocking collectives: 147 us -> none  [body(): total_sq = lax.psum(partial_sq, 'seq')]
    all_gather x1 -> x0, blocking collectives: 90.1 us -> none  [body(): piece = lax.all_gather(decode_mix, 'seq', axis=2, tiled=True)]
    all_to_all x0 -> x2, blocking collectives: none -> 39.9 us  [the longest x1 22.6 us: body(): got = lax.all_to_all(send, 'seq', split_axis=0, concat_axis=0, tiled=True)]
    dot_general x6 -> x0, matrix products: 29.1 us -> none  [the longest x1 13.7 us: one_group(): jnp.einsum('mgnk,bmgk->bmgn', spread, block_sums, precision=highest)]
    convert_element_type x9 -> x0, other arithmetic: 27.8 us -> none  [the longest x2 14.6 us: body(): gated = (query_part.astype(jnp.float32) * conv).astype(jnp.bfloat16)]
    unnamed x21 -> x2, local copies, waits for them, and re-layouts: 27.9 us -> 1.46 us
  transfers between devices with their start and end apart: 5 -> 1, of which waited for: 3 -> 0; matrix products, arithmetic and copies ran while one was open for 32% -> 0% of each run, Pallas kernels for 0% -> 13%
where the time goes in v1:
time: 74.9 us; the launch traced here: 74.5 us
  blocking collectives  39.9 us (53%)
  Pallas kernels  23.4 us (31%)
  starting transfers between devices  7.28 us (10%)
  local copies, waits for them, and re-layouts  1.97 us (3%)
  other arithmetic  1.25 us (2%)
    all_to_all x1, blocking collectives, body(): got = lax.all_to_all(send, 'seq', split_axis=0, concat_axis=0, tiled=True)  22.6 us
    all_to_all x1, blocking collectives, body(): given = lax.all_to_all(back, 'seq', split_axis=0, concat_axis=0, tiled=True)  17.4 us
    pallas_call x1, Pallas kernels, body(): pl.pallas_call(lambda *refs: last_kernel(modes, shard, *refs), grid=(halv...  9.8 us
    pallas_call x1, Pallas kernels, body(): pl.pallas_call(lambda *refs: first_kernel(modes, shard, *refs), grid_spec...  9.17 us
    all_to_all x1, starting transfers between devices, body(): lax.all_to_all(partial, 'chan', split_axis=0, concat_axis=0, tiled=True)  7.28 us
    pallas_call x1, Pallas kernels, body(): pl.pallas_call(lambda *refs: owner_kernel(width, shard, steps, *refs), ou...  2.4 us
    pallas_call x1, Pallas kernels, body(): pl.pallas_call(decode_kernel, grid=(1,), in_specs=[pl.BlockSpec((devices,...  2.04 us
  transfers between devices with their start and end apart: 1, of which 0 were waited for; matrix products, arithmetic and copies ran while one was open for 0% of the time, Pallas kernels for 13%

profile of v1, /device:TPU:1, one launch (start us, length us, event | category | flops | bytes accessed | tf_op | source)
XLA Modules:
  0.0 74.5 jit_solution(6782462464225273541)
XLA Ops:
  0.6 9.2 %first.1 = (f32[2,2,128,8,128]{4,3,2,1,0:T(8,128)}, f32[64,16,128]{2,1,0:T(8,128)}) custom-call(s32[2,4]{1,0:T(2,128)} %refs_0_.1, s32[2]{0:T(128)} %refs_1_.2, bf16[3,2,2048,128]{3,2,1,0:T(8,128)(2,1)} %refs_2_.5, bf16[3,2,2048,128]{3,2,1,0:T(8,128)(2,1)} %refs_2_.5, f32[16,2048]{1,0:T(8,128)} %refs_3_.3, bf16[512,128]{1,0:T(8,128)(2,1)} %refs_5_.1, ...), custom_call_target="tpu_custom_call" | custom-call | tf_op jit(solution)/shard_map/first/pallas_call | solution.py:205
  9.8 22.6 %all_to_all.15.refs_0_ = f32[64,16,128]{2,1,0:T(8,128)} all-to-all(f32[64,16,128]{2,1,0:T(8,128)} %get-tuple-element.4), channel_id=1, replica_groups=mesh['seq'=64,'chan'=4] {'seq'}, dimensions={0} | all-to-all | bytes 1048576 | tf_op jit(solution)/shard_map/all_to_all | solution.py:237
  32.4 2.4 %owner.1 = f32[64,16,128]{2,1,0:T(8,128)} custom-call(f32[64,16,128]{2,1,0:T(8,128)} %all_to_all.15.refs_0_, f32[16,2048]{1,0:T(8,128)} %refs_3_.3, f32[16,2048]{1,0:T(8,128)} %refs_4_.3, f32[16,128]{1,0:T(8,128)} %bitcast.3), custom_call_target="tpu_custom_call" | custom-call | tf_op jit(solution)/shard_map/owner/pallas_call | solution.py:239
  34.8 17.4 %all_to_all.16.refs_0_.mix_ref = f32[64,16,128]{2,1,0:T(8,128)} all-to-all(f32[64,16,128]{2,1,0:T(8,128)} %owner.1), channel_id=1, replica_groups=mesh['seq'=64,'chan'=4] {'seq'}, dimensions={0} | all-to-all | bytes 1048576 | tf_op jit(solution)/shard_map/all_to_all | solution.py:245
  52.1 2.0 %decode.1 = f32[4,8,32]{2,1,0:T(8,128)} custom-call(f32[64,16,128]{2,1,0:T(8,128)} %all_to_all.16.refs_0_.mix_ref, bf16[2048,128]{1,0:T(8,128)(2,1)} %w_ref.1), custom_call_target="tpu_custom_call" | custom-call | tf_op jit(solution)/shard_map/decode/pallas_call | solution.py:247
  54.2 1.4 %reshape.15 = f32[4,1,256]{2,1,0:T(1,128)} reshape(f32[4,8,32]{2,1,0:T(8,128)} %decode.1) | data formatting | bytes 8192
  55.6 7.3 %all-to-all-start.2 = ((f32[4,1,256]{2,1,0:T(1,128)}), f32[4,1,256]{2,1,0:T(1,128)S(1)}, u32[]{:S(2)}, u32[]{:S(2)}) async-start(f32[4,1,256]{2,1,0:T(1,128)} %reshape.15), calls=%async_computation.2 | async-start | bytes 8192 | tf_op jit(solution)/shard_map/all_to_all | solution.py:258
  62.8 9.8 %last.1 = bf16[2,2048,128]{2,1,0:T(8,128)(2,1)} custom-call(f32[64,16,128]{2,1,0:T(8,128)} %all_to_all.16.refs_0_.mix_ref, f32[2,2,128,8,128]{4,3,2,1,0:T(8,128)} %get-tuple-element.5.refs_1_, bf16[3,2,2048,128]{3,2,1,0:T(8,128)(2,1)} %refs_2_.5, f32[16,2048]{1,0:T(8,128)} %refs_3_.3, f32[16,2048]{1,0:T(8,128)} %refs_4_.3, f32[16,128]{1,0:T(8,128)} %bitcast.4), custom_call_target="tpu_custom_call" | custom-call | flops 33554432 | bytes 4194304 | tf_op jit(solution)/shard_map/last/pallas_call | solution.py:261
  72.6 0.0 all-to-all-done.2
  72.6 0.5 broadcast
  73.2 0.7 reduce
  73.8 0.1 reshape.16
  73.9 0.6 reduce_sum.9
Async XLA Ops:
  55.6 17.1 %all-to-all-start.2 = ((f32[4,1,256]{2,1,0:T(1,128)}), f32[4,1,256]{2,1,0:T(1,128)S(1)}, u32[]{:S(2)}, u32[]{:S(2)}) async-start(f32[4,1,256]{2,1,0:T(1,128)} %reshape.15), calls=%async_computation.2 | async-start | bytes 8192 | tf_op jit(solution)/shard_map/all_to_all | solution.py:258

commit v2 on v1

v2 whole, which is shorter than its diff:
```python
import jax
import jax.numpy as jnp
from jax import lax
from jax.experimental import pallas as pl
from jax.experimental.pallas import tpu as pltpu
from jax.sharding import PartitionSpec as P

LANES = 128
SUB = 8
GROUPS = 4
PAD = 9
PITCH = 132
EPS = 1e-05
VMEM_LIMIT = 8 * 2**20
WIDE_LIMIT = 60 * 2**20


def quarter_of(shape):
    return lax.broadcasted_iota(jnp.int32, shape, len(shape) - 1) // 32


def spread(tiles):
    lane = lax.broadcasted_iota(jnp.int32, tiles[0].shape, 1)
    low, even = lane < 64, (lane // 32) % 2 == 0
    made = list(tiles)
    for r in range(2):
        a, b = tiles[r], tiles[r + 2]
        made[r] = jnp.where(low, a, pltpu.roll(b, 64, 1))
        made[r + 2] = jnp.where(low, pltpu.roll(a, 64, 1), b)
    for r in (0, 2):
        a, b = made[r], made[r + 1]
        made[r] = jnp.where(even, a, pltpu.roll(b, 32, 1))
        made[r + 1] = jnp.where(even, pltpu.roll(a, 96, 1), b)
    return made


def rounded(x):
    return x.astype(jnp.bfloat16).astype(jnp.float32)


def pairs_sum(terms):
    while len(terms) > 1:
        terms = [x + y for x, y in zip(terms[::2], terms[1::2])] + terms[len(terms) // 2 * 2:]
    return terms[0]


def fill(scratch, ref, batch, fn):
    modes = ref.shape[0]
    for g in range(GROUPS):
        values = fn(ref[:, g * LANES:(g + 1) * LANES])
        for b in range(batch):
            scratch[pl.ds(b * GROUPS + g, modes, stride=PAD), :] = values


def tiles_of(scratch, modes):
    return [scratch[m * PAD:m * PAD + SUB, :] for m in range(modes)]


def first_kernel(modes, shard, tokens, offsets, k_ref, v_ref, rate_ref, emb_ref, gain_ref, w_ref,
                 u_out, send, trans, decay, state, x16, squares):
    part = pl.program_id(0)
    position = lax.axis_index("seq") * shard + lax.broadcasted_iota(jnp.int32, (LANES, shard), 1)
    batch = k_ref.shape[1]
    steps = tokens.shape[1]
    count = batch * steps

    @pl.when(part == 0)
    def _():
        vocab = emb_ref.shape[0]
        row = lax.broadcasted_iota(jnp.int32, (16, vocab), 0)
        wanted = jnp.full((16, vocab), -1, jnp.int32)
        for t in range(count):
            wanted = jnp.where(row == t, tokens[t // steps, t % steps], wanted)
        hot = (lax.broadcasted_iota(jnp.int32, (16, vocab), 1) == wanted).astype(jnp.float32)
        x = jnp.dot(hot.astype(jnp.bfloat16), emb_ref[...], preferred_element_type=jnp.float32)[:SUB]
        squares[...] = jnp.broadcast_to(jnp.sum(x * x, axis=1, keepdims=True), (SUB, LANES))
        scaled = x * gain_ref[...]
        high = rounded(scaled)
        x16[...] = jnp.concatenate([high, scaled - high], axis=0).astype(jnp.bfloat16)

    fill(decay, rate_ref, batch, lambda x: jnp.exp(-x))
    for g in range(GROUPS):
        for b in range(batch):
            rows = slice(g * LANES, (g + 1) * LANES)
            product = k_ref[0, b, rows].astype(jnp.float32) * v_ref[0, b, rows].astype(jnp.float32)
            u = rounded(jnp.where(position >= offsets[b], product, 0.0))
            trans[pl.ds((b * GROUPS + g) * PITCH, shard), :] = u.T

    rates = tiles_of(decay, modes)

    def step(t, held):
        u = trans[pl.ds(t, SUB, stride=PITCH), :]
        u_out[0, t] = u
        return tuple(rates[m] * held[m] + u for m in range(modes))

    zero = jnp.zeros((SUB, LANES), jnp.float32)
    held = lax.fori_loop(0, shard, step, (zero,) * modes, unroll=4)
    for m in range(modes):
        state[m * PAD:m * PAD + SUB, :] = held[m]

    terms = []
    for i in range(3):
        both = jnp.dot(x16[...], w_ref[i], preferred_element_type=jnp.float32)
        terms.append(both[:SUB] + both[SUB:])
    for g in range(GROUPS):
        ends = [state[pl.ds((r // 2) * GROUPS + g + (r % 2) * SUB * PAD, SUB, stride=PAD), :] for r in range(4)]
        ends = spread(ends)
        parts = spread([t[:, g * LANES:(g + 1) * LANES] for t in terms] + [squares[...]])
        for q in range(4):
            send[g * 4 + q, :SUB] = ends[q]
            send[g * 4 + q, SUB:] = parts[q]


def local_kernel(modes, shard, u_ref, rate_ref, res_ref, skip_ref, out, decay, weight):
    batch = SUB // GROUPS
    fill(decay, rate_ref, batch, lambda x: jnp.exp(-x))
    fill(weight, res_ref, batch, lambda x: x)
    rates, weights = tiles_of(decay, modes), tiles_of(weight, modes)
    skip = jnp.concatenate([skip_ref[0]] * batch, axis=0)

    def step(t, held):
        u = u_ref[0, t]
        held = tuple(rates[m] * held[m] + u for m in range(modes))
        out[0, t] = pairs_sum([weights[m] * held[m] for m in range(modes)] + [skip * u])
        return held

    zero = jnp.zeros((SUB, LANES), jnp.float32)
    lax.fori_loop(0, shard, step, (zero,) * modes, unroll=2)


def owner_kernel(width, shard, steps, got, rate_ref, res_ref, skip_ref, back):
    owner = lax.axis_index("seq")
    group, part = owner // 4, owner % 4
    turn = (LANES - 32 * part) % LANES
    quarter = quarter_of((SUB, LANES))

    def four(a, b, c, d):
        b, c, d = pltpu.roll(b, 32, 1), pltpu.roll(c, 64, 1), pltpu.roll(d, 96, 1)
        return jnp.where(quarter == 0, a, jnp.where(quarter == 1, b, jnp.where(quarter == 2, c, d)))

    def packed(ref):
        own = ref[:, pl.ds(pl.multiple_of(group * LANES, LANES), LANES)]
        own = pltpu.roll(own, turn, 1)
        low, high = own[:SUB], own[SUB:]
        return four(low, high, low, high)

    rate = packed(rate_ref)
    res = packed(res_ref)
    jump = jnp.exp(-rate * shard)
    carried = jnp.zeros((SUB, LANES), jnp.float32)
    total = jnp.zeros((SUB, LANES), jnp.float32)
    for i in range(got.shape[0]):
        back[i, :SUB] = carried
        carried = jump * carried + got[i, :SUB]
        total = total + got[i, SUB:]
    scale = lax.rsqrt(pltpu.roll(total, 32, 1) / width + EPS)
    query = rounded(total * scale)
    key = rounded(pltpu.roll(total, 96, 1) * scale)
    value = rounded(pltpu.roll(total, 64, 1) * scale)
    weight = rounded(key * value)
    weight = four(weight, weight, weight, weight)
    skip = jnp.broadcast_to(skip_ref[pl.ds(group, 1), :], (SUB, LANES))
    skip = pltpu.roll(skip, turn, 1)
    skip = four(skip, skip, skip, skip)
    decay = jnp.exp(-rate)
    row = lax.broadcasted_iota(jnp.int32, (SUB, LANES), 0)
    conv = jnp.zeros((SUB, LANES), jnp.float32)
    for s in range(steps):
        first = jnp.broadcast_to(weight[s:s + 1], (SUB, LANES))
        second = jnp.broadcast_to(weight[steps + s:steps + s + 1], (SUB, LANES))
        w = jnp.where(quarter < 2, first, second)
        carried = decay * carried + w
        summed = jnp.broadcast_to(jnp.sum(res * carried, axis=0, keepdims=True), (SUB, LANES))
        summed = summed + pltpu.roll(summed, 96, 1) + skip * w
        conv = jnp.where(row == s, summed, conv)
        conv = jnp.where(row == steps + s, pltpu.roll(summed, 64, 1), conv)
    mix = rounded(query * conv)
    for i in range(got.shape[0]):
        back[i, SUB:] = mix


def decode_kernel(steps, mix_ref, w_ref, out):
    quarter = quarter_of((SUB, LANES))
    pieces = []
    for g in range(mix_ref.shape[0] // 4):
        tile = mix_ref[g * 4]
        for q in range(1, 4):
            tile = jnp.where(quarter == q, pltpu.roll(mix_ref[g * 4 + q], 32 * q, 1), tile)
        pieces.append(tile)
    mix = jnp.concatenate(pieces, axis=1).astype(jnp.bfloat16)
    summed = jnp.dot(mix, w_ref[...], preferred_element_type=jnp.float32)
    rows = SUB // steps
    ordered = [jnp.concatenate([summed[b * steps + s:b * steps + s + 1] for b in range(rows)], axis=0) for s in range(steps)]
    for k, tile in enumerate(spread(ordered)):
        out[k] = tile


def finish_kernel(steps, ref, out):
    total = ref[0] + ref[1] + ref[2] + ref[3]
    for s in range(steps):
        out[:, s, :] = total[:, s * 32:(s + 1) * 32].astype(jnp.bfloat16)


def last_kernel(modes, shard, carry_ref, near_ref, q_ref, rate_ref, res_ref, out, trans, decay, weight, state):
    batch = q_ref.shape[1]
    fill(decay, rate_ref, batch, lambda x: jnp.exp(-x))
    fill(weight, res_ref, batch, lambda x: x)
    for g in range(GROUPS):
        tiles = spread([carry_ref[g * 4 + q] for q in range(4)])
        for r in range(4):
            state[pl.ds((r // 2) * GROUPS + g + (r % 2) * SUB * PAD, SUB, stride=PAD), :] = tiles[r]
    rates, weights = tiles_of(decay, modes), tiles_of(weight, modes)

    def step(t, held):
        trans[pl.ds(t, SUB, stride=PITCH), :] = pairs_sum(list(held) + [near_ref[0, t]])
        return tuple(rates[m] * held[m] for m in range(modes))

    held = tuple(weights[m] * (rates[m] * state[m * PAD:m * PAD + SUB, :]) for m in range(modes))
    lax.fori_loop(0, shard, step, held, unroll=4)
    for b in range(batch):
        for g in range(GROUPS):
            rows = slice(g * LANES, (g + 1) * LANES)
            conv = trans[pl.ds((b * GROUPS + g) * PITCH, shard), :].T
            out[b, rows] = (q_ref[0, b, rows].astype(jnp.float32) * conv).astype(jnp.bfloat16)


def body(features, offsets, tokens, decay_rate, residue, skip_weight, embedding, norm_gain, dec_weight, out_weight):
    _, batch, chans, shard = features.shape
    modes = decay_rate.shape[0]
    steps = tokens.shape[1]
    vocab = embedding.shape[0]
    devices = lax.axis_size("seq")
    width = devices * norm_gain.shape[0]
    block = GROUPS * LANES
    parts = chans // block
    f32 = jnp.float32
    gain = norm_gain.reshape(1, -1)
    skip = skip_weight.reshape(chans // LANES, LANES)
    per_mode = pltpu.VMEM((modes * PAD, LANES), f32)
    across = pltpu.VMEM((SUB * PITCH, LANES), f32)
    by_part = pl.BlockSpec((modes, block), lambda h, *_: (0, h))
    in_time = pl.BlockSpec((1, shard, SUB, LANES), lambda h, *_: (h, 0, 0, 0))
    wide = pltpu.CompilerParams(vmem_limit_bytes=WIDE_LIMIT)
    limit = pltpu.CompilerParams(vmem_limit_bytes=VMEM_LIMIT)

    u_t, send = pl.pallas_call(
        lambda *refs: first_kernel(modes, shard, *refs),
        grid_spec=pltpu.PrefetchScalarGridSpec(
            num_scalar_prefetch=2,
            grid=(parts,),
            in_specs=[
                pl.BlockSpec((1, batch, block, shard), lambda h, *_: (1, 0, h, 0)),
                pl.BlockSpec((1, batch, block, shard), lambda h, *_: (2, 0, h, 0)),
                by_part,
                pl.BlockSpec((vocab, shard), lambda h, *_: (0, 0)),
                pl.BlockSpec((1, shard), lambda h, *_: (0, 0)),
                pl.BlockSpec((3, shard, block), lambda h, *_: (0, 0, h)),
            ],
            out_specs=[in_time, pl.BlockSpec((devices // parts, 2 * SUB, LANES), lambda h, *_: (h, 0, 0))],
            scratch_shapes=[across, per_mode, per_mode, pltpu.VMEM((16, shard), jnp.bfloat16), pltpu.VMEM((SUB, LANES), f32)],
        ),
        out_shape=[
            jax.ShapeDtypeStruct((parts, shard, SUB, LANES), f32),
            jax.ShapeDtypeStruct((devices, 2 * SUB, LANES), f32),
        ],
        compiler_params=wide,
        name="first",
    )(tokens, offsets, features, features, decay_rate, embedding, gain, dec_weight)

    got = lax.all_to_all(send, "seq", split_axis=0, concat_axis=0, tiled=True)

    near = pl.pallas_call(
        lambda *refs: local_kernel(modes, shard, *refs),
        grid=(parts,),
        in_specs=[in_time, by_part, by_part, pl.BlockSpec((1, GROUPS, LANES), lambda h: (h, 0, 0))],
        out_specs=in_time,
        out_shape=jax.ShapeDtypeStruct((parts, shard, SUB, LANES), f32),
        scratch_shapes=[per_mode, per_mode],
        compiler_params=wide,
        cost_estimate=pl.CostEstimate(flops=2**25, bytes_accessed=2**22, transcendentals=0),
        name="local",
    )(u_t, decay_rate, residue, skip.reshape(parts, GROUPS, LANES))

    got, near = lax.optimization_barrier((got, near))
    back = pl.pallas_call(
        lambda *refs: owner_kernel(width, shard, steps, *refs),
        out_shape=jax.ShapeDtypeStruct((devices, 2 * SUB, LANES), f32),
        compiler_params=limit,
        name="owner",
    )(got, decay_rate, residue, skip)

    given = lax.all_to_all(back, "seq", split_axis=0, concat_axis=0, tiled=True)

    partial = pl.pallas_call(
        lambda *refs: decode_kernel(steps, *refs),
        grid=(1,),
        in_specs=[
            pl.BlockSpec((devices, SUB, LANES), lambda i: (0, 1, 0)),
            pl.BlockSpec((chans, LANES), lambda i: (0, 0)),
        ],
        out_specs=pl.BlockSpec((4, batch, LANES), lambda i: (0, 0, 0)),
        out_shape=jax.ShapeDtypeStruct((4, batch, LANES), f32),
        compiler_params=limit,
        name="decode",
    )(given, out_weight)
    pieces = lax.all_to_all(partial, "chan", split_axis=0, concat_axis=0, tiled=True)

    mixed = pl.pallas_call(
        lambda *refs: last_kernel(modes, shard, *refs),
        grid=(parts,),
        in_specs=[
            pl.BlockSpec((devices // parts, SUB, LANES), lambda h: (h, 0, 0)),
            in_time,
            pl.BlockSpec((1, batch, block, shard), lambda h: (0, 0, h, 0)),
            by_part,
            by_part,
        ],
        out_specs=pl.BlockSpec((batch, block, shard), lambda h: (0, h, 0)),
        out_shape=jax.ShapeDtypeStruct((batch, chans, shard), jnp.bfloat16),
        scratch_shapes=[across, per_mode, per_mode, per_mode],
        compiler_params=wide,
        cost_estimate=pl.CostEstimate(flops=2**25, bytes_accessed=2**22, transcendentals=0),
        name="last",
    )(given, near, features, decay_rate, residue)

    decoded = pl.pallas_call(
        lambda *refs: finish_kernel(steps, *refs),
        out_shape=jax.ShapeDtypeStruct((batch, steps, 32), jnp.bfloat16),
        compiler_params=limit,
        name="finish",
    )(pieces)
    return (mixed, decoded)


def solution(mesh):
    placed = (
        P(None, None, "chan", "seq"),
        P(),
        P(),
        P(None, "chan"),
        P(None, "chan"),
        P("chan"),
        P(None, "seq"),
        P("seq"),
        P(None, "seq", "chan"),
        P("chan", "seq"),
    )
    return jax.shard_map(
        body,
        mesh=mesh,
        in_specs=placed,
        out_specs=(P(None, "chan", "seq"), P(None, None, ("seq", "chan"))),
        check_vma=False,
    )
```

time: 74.9 us -> 63.8 us (0.85)
  blocking collectives: 39.9 us -> 16.7 us
  starting transfers between devices: 7.28 us -> 17.6 us
  waiting for transfers between devices: 0.01 us -> 4.74 us
  local copies, waits for them, and re-layouts: 1.97 us -> 0.03 us
  other arithmetic: 1.25 us -> 0 us
    all_to_all x1 -> x0, blocking collectives: 22.6 us -> none  [body(): got = lax.all_to_all(send, 'seq', split_axis=0, concat_axis=0, tiled=True)]
    all_to_all x0 -> x1, starting transfers between devices: none -> 10.3 us  [body(): got = lax.all_to_all(send, 'seq', split_axis=0, concat_axis=0, tiled=True)]
    all_to_all x0 -> x1, waiting for transfers between devices: none -> 4.34 us  [body(): got = lax.all_to_all(send, 'seq', split_axis=0, concat_axis=0, tiled=True)]
    pallas_call x2 -> x4, Pallas kernels: 11.8 us -> 15.6 us  [the longest x1 7.77 us: body(): pl.pallas_call(lambda *refs: local_kernel(modes, shard, *refs), grid=(par...]
    pallas_call x1, Pallas kernels: 2.4 us -> 0.47 us  [body(): pl.pallas_call(lambda *refs: owner_kernel(width, shard, steps, *refs), ou...]
    pallas_call x1, Pallas kernels: 9.17 us -> 7.57 us  [body(): pl.pallas_call(lambda *refs: first_kernel(modes, shard, *refs), grid_spec...]
    unnamed x2 -> x10, local copies, waits for them, and re-layouts: 1.46 us -> 0.03 us
  transfers between devices with their start and end apart: 1 -> 2, of which waited for: 0 -> 2; matrix products, arithmetic and copies ran while one was open for 0% -> 0% of each run, Pallas kernels for 13% -> 22%
where the time goes in v2:
time: 63.8 us; the launch traced here: 63.4 us
  Pallas kernels  23.6 us (37%)
  starting transfers between devices  17.6 us (28%)
  blocking collectives  16.7 us (26%)
  waiting for transfers between devices  4.74 us (7%)
  between operations  0.68 us (1%)
    all_to_all x1, blocking collectives, body(): given = lax.all_to_all(back, 'seq', split_axis=0, concat_axis=0, tiled=True)  16.7 us
    all_to_all x1, starting transfers between devices, body(): got = lax.all_to_all(send, 'seq', split_axis=0, concat_axis=0, tiled=True)  10.3 us
    pallas_call x1, Pallas kernels, body(): pl.pallas_call(lambda *refs: local_kernel(modes, shard, *refs), grid=(par...  7.77 us
    pallas_call x1, Pallas kernels, body(): pl.pallas_call(lambda *refs: first_kernel(modes, shard, *refs), grid_spec...  7.57 us
    all_to_all x1, starting transfers between devices, body(): lax.all_to_all(partial, 'chan', split_axis=0, concat_axis=0, tiled=True)  7.28 us
    pallas_call x1, Pallas kernels, body(): pl.pallas_call(lambda *refs: last_kernel(modes, shard, *refs), grid=(part...  6.16 us
    all_to_all x1, waiting for transfers between devices, body(): got = lax.all_to_all(send, 'seq', split_axis=0, concat_axis=0, tiled=True)  4.34 us
  transfers between devices with their start and end apart: 2, of which 2 were waited for; matrix products, arithmetic and copies ran while one was open for 0% of the time, Pallas kernels for 22%

profile of v2, /device:TPU:1, one launch (start us, length us, event | category | flops | bytes accessed | tf_op | source)
XLA Modules:
  0.0 63.4 jit_solution(16242543493046578936)
XLA Ops:
  0.6 7.6 %first.1 = (f32[4,128,8,128]{3,2,1,0:T(8,128)}, f32[64,16,128]{2,1,0:T(8,128)}) custom-call(s32[2,4]{1,0:T(2,128)} %refs_0_.1, s32[2]{0:T(128)} %refs_1_.4, bf16[3,2,2048,128]{3,2,1,0:T(8,128)(2,1)} %refs_2_.7, bf16[3,2,2048,128]{3,2,1,0:T(8,128)(2,1)} %refs_2_.7, f32[16,2048]{1,0:T(8,128)} %refs_3_.3, bf16[512,128]{1,0:T(8,128)(2,1)} %refs_5_.1, ...), custom_call_target="tpu_custom_call" | custom-call | tf_op jit(solution)/shard_map/first/pallas_call | solution.py:246
  8.2 10.3 %all-to-all-start = ((f32[64,16,128]{2,1,0:T(8,128)}), f32[64,16,128]{2,1,0:T(8,128)S(1)}, u32[]{:S(2)}, u32[]{:S(2)}) async-start(f32[64,16,128]{2,1,0:T(8,128)} %get-tuple-element.6), calls=%async_computation | async-start | bytes 1048576 | tf_op jit(solution)/shard_map/all_to_all | solution.py:270
  18.5 0.0 copy-start.1
  18.6 0.0 copy-start.2
  18.6 0.0 copy-start.4
  18.6 7.8 %local.1.refs_1_ = f32[4,128,8,128]{3,2,1,0:T(8,128)} custom-call(f32[4,128,8,128]{3,2,1,0:T(8,128)} %get-tuple-element.7.refs_0_, f32[16,2048]{1,0:T(8,128)} %refs_3_.3, f32[16,2048]{1,0:T(8,128)} %refs_4_.3, f32[4,4,128]{2,1,0:T(4,128)} %bitcast.3), custom_call_target="tpu_custom_call" | custom-call | flops 33554432 | bytes 4194304 | tf_op jit(solution)/shard_map/local/pallas_call | solution.py:272
  26.4 0.0 copy-start.3
  26.4 4.3 %all-to-all-done.refs_0_ = f32[64,16,128]{2,1,0:T(8,128)S(1)} async-done(((f32[64,16,128]{2,1,0:T(8,128)}), f32[64,16,128]{2,1,0:T(8,128)S(1)}, u32[]{:S(2)}, u32[]{:S(2)}) %all-to-all-start) | async-done | bytes 524320 | tf_op jit(solution)/shard_map/all_to_all | solution.py:270
  30.7 0.0 copy-done.1
  30.7 0.0 copy-done.2
  30.7 0.0 copy-done.4
  30.7 0.5 owner.1
  31.2 16.7 %all_to_all.15.refs_0_ = f32[64,16,128]{2,1,0:T(8,128)S(1)} all-to-all(f32[64,16,128]{2,1,0:T(8,128)S(1)} %owner.1), channel_id=1, replica_groups=mesh['seq'=64,'chan'=4] {'seq'}, dimensions={0} | all-to-all | bytes 1048576 | tf_op jit(solution)/shard_map/all_to_all | solution.py:292
  47.9 0.0 copy-done.3
  47.9 0.0 copy-start
  47.9 1.0 %decode.1 = f32[4,2,128]{2,1,0:T(2,128)} custom-call(f32[64,16,128]{2,1,0:T(8,128)S(1)} %all_to_all.15.refs_0_, bf16[2048,128]{1,0:T(8,128)(2,1)S(1)} %copy-done.3), custom_call_target="tpu_custom_call" | custom-call | tf_op jit(solution)/shard_map/decode/pallas_call | solution.py:294
  48.9 7.3 %all-to-all-start.2 = ((f32[4,2,128]{2,1,0:T(2,128)}), f32[4,2,128]{2,1,0:T(2,128)S(1)}, u32[]{:S(2)}, u32[]{:S(2)}) async-start(f32[4,2,128]{2,1,0:T(2,128)} %decode.1), calls=%async_computation.2 | async-start | bytes 8192 | tf_op jit(solution)/shard_map/all_to_all | solution.py:306
  56.2 0.0 copy-done
  56.2 6.2 %last.1 = bf16[2,2048,128]{2,1,0:T(8,128)(2,1)} custom-call(f32[64,16,128]{2,1,0:T(8,128)} %copy-done, f32[4,128,8,128]{3,2,1,0:T(8,128)} %local.1.refs_1_, bf16[3,2,2048,128]{3,2,1,0:T(8,128)(2,1)} %refs_2_.7, f32[16,2048]{1,0:T(8,128)} %refs_3_.3, f32[16,2048]{1,0:T(8,128)} %refs_4_.3), custom_call_target="tpu_custom_call" | custom-call | flops 33554432 | bytes 4194304 | tf_op jit(solution)/shard_map/last/pallas_call | solution.py:308
  62.3 0.4 all-to-all-done.2.refs_0_
  62.7 0.7 %finish.1 = bf16[2,4,32]{2,1,0:T(4,128)(2,1)} custom-call(f32[4,2,128]{2,1,0:T(2,128)S(1)} %all-to-all-done.2.refs_0_), custom_call_target="tpu_custom_call" | custom-call | tf_op jit(solution)/shard_map/finish/pallas_call | solution.py:326
Async XLA Ops:
  8.2 22.5 %all-to-all-start = ((f32[64,16,128]{2,1,0:T(8,128)}), f32[64,16,128]{2,1,0:T(8,128)S(1)}, u32[]{:S(2)}, u32[]{:S(2)}) async-start(f32[64,16,128]{2,1,0:T(8,128)} %get-tuple-element.6), calls=%async_computation | async-start | bytes 1048576 | tf_op jit(solution)/shard_map/all_to_all | solution.py:270
  18.5 12.2 %copy-start.1 = (f32[16,2048]{1,0:T(8,128)S(1)}, f32[16,2048]{1,0:T(8,128)}, u32[]{:S(2)}) copy-start(f32[16,2048]{1,0:T(8,128)} %refs_3_.3) | copy-start | bytes 393220
  18.6 12.1 %copy-start.2 = (f32[16,2048]{1,0:T(8,128)S(1)}, f32[16,2048]{1,0:T(8,128)}, u32[]{:S(2)}) copy-start(f32[16,2048]{1,0:T(8,128)} %refs_4_.3) | copy-start | bytes 393220
  18.6 12.1 %copy-start.4 = (f32[2048]{0:T(1024)S(1)}, f32[2048]{0:T(1024)}, u32[]{:S(2)}) copy-start(f32[2048]{0:T(1024)} %param.15) | copy-start | bytes 24580
  26.4 21.5 %copy-start.3 = (bf16[2048,128]{1,0:T(8,128)(2,1)S(1)}, bf16[2048,128]{1,0:T(8,128)(2,1)}, u32[]{:S(2)}) copy-start(bf16[2048,128]{1,0:T(8,128)(2,1)} %refs_1_.7) | copy-start | bytes 1572868
  47.9 8.3 %copy-start = (f32[64,16,128]{2,1,0:T(8,128)}, f32[64,16,128]{2,1,0:T(8,128)S(1)}, u32[]{:S(2)}) copy-start(f32[64,16,128]{2,1,0:T(8,128)S(1)} %all_to_all.15.refs_0_) | copy-start | bytes 1572868
  48.9 13.8 %all-to-all-start.2 = ((f32[4,2,128]{2,1,0:T(2,128)}), f32[4,2,128]{2,1,0:T(2,128)S(1)}, u32[]{:S(2)}, u32[]{:S(2)}) async-start(f32[4,2,128]{2,1,0:T(2,128)} %decode.1), calls=%async_computation.2 | async-start | bytes 8192 | tf_op jit(solution)/shard_map/all_to_all | solution.py:306

commit v3 on v2

--- a/solution.py
+++ b/solution.py
@@ -57,7 +57,7 @@
 
 
 def first_kernel(modes, shard, tokens, offsets, k_ref, v_ref, rate_ref, emb_ref, gain_ref, w_ref,
-                 u_out, send, trans, decay, state, x16, squares):
+                 u_out, send, trans, decay, state, x16, squares, sums):
     part = pl.program_id(0)
     position = lax.axis_index("seq") * shard + lax.broadcasted_iota(jnp.int32, (LANES, shard), 1)
     batch = k_ref.shape[1]
@@ -86,6 +86,15 @@
             u = rounded(jnp.where(position >= offsets[b], product, 0.0))
             trans[pl.ds((b * GROUPS + g) * PITCH, shard), :] = u.T
 
+    terms = []
+    for i in range(3):
+        both = jnp.dot(x16[...], w_ref[i], preferred_element_type=jnp.float32)
+        terms.append(both[:SUB] + both[SUB:])
+    for g in range(GROUPS):
+        parts = spread([t[:, g * LANES:(g + 1) * LANES] for t in terms] + [squares[...]])
+        for q in range(4):
+            sums[g * 4 + q] = parts[q]
+
     rates = tiles_of(decay, modes)
 
     def step(t, held):
@@ -98,17 +107,10 @@
     for m in range(modes):
         state[m * PAD:m * PAD + SUB, :] = held[m]
 
-    terms = []
-    for i in range(3):
-        both = jnp.dot(x16[...], w_ref[i], preferred_element_type=jnp.float32)
-        terms.append(both[:SUB] + both[SUB:])
     for g in range(GROUPS):
         ends = [state[pl.ds((r // 2) * GROUPS + g + (r % 2) * SUB * PAD, SUB, stride=PAD), :] for r in range(4)]
-        ends = spread(ends)
-        parts = spread([t[:, g * LANES:(g + 1) * LANES] for t in terms] + [squares[...]])
-        for q in range(4):
-            send[g * 4 + q, :SUB] = ends[q]
-            send[g * 4 + q, SUB:] = parts[q]
+        for q, tile in enumerate(spread(ends)):
+            send[g * 4 + q] = jnp.concatenate([tile, sums[g * 4 + q]], axis=0).astype(jnp.bfloat16)
 
 
 def local_kernel(modes, shard, u_ref, rate_ref, res_ref, skip_ref, out, decay, weight):
@@ -128,6 +130,10 @@
     lax.fori_loop(0, shard, step, (zero,) * modes, unroll=2)
 
 
+def by_step(x, s, steps, rows):
+    return jnp.concatenate([x[b * steps + s:b * steps + s + 1] for b in range(rows)], axis=0)
+
+
 def owner_kernel(width, shard, steps, got, rate_ref, res_ref, skip_ref, back):
     owner = lax.axis_index("seq")
     group, part = owner // 4, owner % 4
@@ -136,6 +142,7 @@
 
     def four(a, b, c, d):
         b, c, d = pltpu.roll(b, 32, 1), pltpu.roll(c, 64, 1), pltpu.roll(d, 96, 1)
+        quarter = quarter_of(a.shape)
         return jnp.where(quarter == 0, a, jnp.where(quarter == 1, b, jnp.where(quarter == 2, c, d)))
 
     def packed(ref):
@@ -150,9 +157,12 @@
     carried = jnp.zeros((SUB, LANES), jnp.float32)
     total = jnp.zeros((SUB, LANES), jnp.float32)
     for i in range(got.shape[0]):
-        back[i, :SUB] = carried
-        carried = jump * carried + got[i, :SUB]
-        total = total + got[i, SUB:]
+        both = got[i].astype(jnp.float32)
+        sent = carried.astype(jnp.bfloat16)
+        for n in range(4):
+            back[i, n] = sent[2 * n:2 * n + 2]
+        carried = jump * carried + both[:SUB]
+        total = total + both[SUB:]
     scale = lax.rsqrt(pltpu.roll(total, 32, 1) / width + EPS)
     query = rounded(total * scale)
     key = rounded(pltpu.roll(total, 96, 1) * scale)
@@ -175,38 +185,39 @@
         conv = jnp.where(row == s, summed, conv)
         conv = jnp.where(row == steps + s, pltpu.roll(summed, 64, 1), conv)
     mix = rounded(query * conv)
+    rows = SUB // steps
+    mix = four(*[by_step(mix, s, steps, rows) for s in range(steps)]).astype(jnp.bfloat16)
     for i in range(got.shape[0]):
-        back[i, SUB:] = mix
-
-
-def decode_kernel(steps, mix_ref, w_ref, out):
-    quarter = quarter_of((SUB, LANES))
+        back[i, 4] = mix
+
+
+def decode_kernel(mix_ref, w_ref, out):
     pieces = []
     for g in range(mix_ref.shape[0] // 4):
-        tile = mix_ref[g * 4]
-        for q in range(1, 4):
-            tile = jnp.where(quarter == q, pltpu.roll(mix_ref[g * 4 + q], 32 * q, 1), tile)
-        pieces.append(tile)
+        pieces.append(jnp.concatenate(spread([mix_ref[g * 4 + q, 0].astype(jnp.float32) for q in range(4)]), axis=0))
     mix = jnp.concatenate(pieces, axis=1).astype(jnp.bfloat16)
-    summed = jnp.dot(mix, w_ref[...], preferred_element_type=jnp.float32)
+    out[...] = jnp.dot(mix, w_ref[...], preferred_element_type=jnp.float32)
+
+
+def add_kernel(a, b, out):
+    out[...] = a[...] + b[...]
+
+
+def finish_kernel(steps, a, b, out):
+    total = pltpu.roll(a[...] + b[...], (LANES - 32 * lax.axis_index("chan")) % LANES, 1)
     rows = SUB // steps
-    ordered = [jnp.concatenate([summed[b * steps + s:b * steps + s + 1] for b in range(rows)], axis=0) for s in range(steps)]
-    for k, tile in enumerate(spread(ordered)):
-        out[k] = tile
-
-
-def finish_kernel(steps, ref, out):
-    total = ref[0] + ref[1] + ref[2] + ref[3]
     for s in range(steps):
-        out[:, s, :] = total[:, s * 32:(s + 1) * 32].astype(jnp.bfloat16)
-
-
-def last_kernel(modes, shard, carry_ref, near_ref, q_ref, rate_ref, res_ref, out, trans, decay, weight, state):
+        out[:, s, :] = total[s * rows:(s + 1) * rows, :32].astype(jnp.bfloat16)
+
+
+def last_kernel(modes, shard, carry_ref, near_ref, q_ref, rate_ref, res_ref, *rest):
+    out, trans, decay, weight, state = rest[-5:]
     batch = q_ref.shape[1]
     fill(decay, rate_ref, batch, lambda x: jnp.exp(-x))
     fill(weight, res_ref, batch, lambda x: x)
     for g in range(GROUPS):
-        tiles = spread([carry_ref[g * 4 + q] for q in range(4)])
+        tiles = [jnp.concatenate([carry_ref[g * 4 + q, n].astype(jnp.float32) for n in range(4)], axis=0) for q in range(4)]
+        tiles = spread(tiles)
         for r in range(4):
             state[pl.ds((r // 2) * GROUPS + g + (r % 2) * SUB * PAD, SUB, stride=PAD), :] = tiles[r]
     rates, weights = tiles_of(decay, modes), tiles_of(weight, modes)
@@ -257,11 +268,11 @@
                 pl.BlockSpec((3, shard, block), lambda h, *_: (0, 0, h)),
             ],
             out_specs=[in_time, pl.BlockSpec((devices // parts, 2 * SUB, LANES), lambda h, *_: (h, 0, 0))],
-            scratch_shapes=[across, per_mode, per_mode, pltpu.VMEM((16, shard), jnp.bfloat16), pltpu.VMEM((SUB, LANES), f32)],
+            scratch_shapes=[across, per_mode, per_mode, pltpu.VMEM((16, shard), jnp.bfloat16), pltpu.VMEM((SUB, LANES), f32), pltpu.VMEM((GROUPS * 4, SUB, LANES), f32)],
         ),
         out_shape=[
             jax.ShapeDtypeStruct((parts, shard, SUB, LANES), f32),
-            jax.ShapeDtypeStruct((devices, 2 * SUB, LANES), f32),
+            jax.ShapeDtypeStruct((devices, 2 * SUB, LANES), jnp.bfloat16),
         ],
         compiler_params=wide,
         name="first",
@@ -269,66 +280,93 @@
 
     got = lax.all_to_all(send, "seq", split_axis=0, concat_axis=0, tiled=True)
 
-    near = pl.pallas_call(
-        lambda *refs: local_kernel(modes, shard, *refs),
-        grid=(parts,),
-        in_specs=[in_time, by_part, by_part, pl.BlockSpec((1, GROUPS, LANES), lambda h: (h, 0, 0))],
-        out_specs=in_time,
-        out_shape=jax.ShapeDtypeStruct((parts, shard, SUB, LANES), f32),
-        scratch_shapes=[per_mode, per_mode],
-        compiler_params=wide,
-        cost_estimate=pl.CostEstimate(flops=2**25, bytes_accessed=2**22, transcendentals=0),
-        name="local",
-    )(u_t, decay_rate, residue, skip.reshape(parts, GROUPS, LANES))
-
-    got, near = lax.optimization_barrier((got, near))
+    halved = parts // 2
+
+    def local(first, rate):
+        shifted = pl.BlockSpec((modes, block), lambda h: (0, h + first))
+        return pl.pallas_call(
+            lambda *refs: local_kernel(modes, shard, *refs),
+            grid=(halved,),
+            in_specs=[
+                pl.BlockSpec((1, shard, SUB, LANES), lambda h: (h + first, 0, 0, 0)),
+                shifted,
+                shifted,
+                pl.BlockSpec((1, GROUPS, LANES), lambda h: (h + first, 0, 0)),
+            ],
+            out_specs=in_time,
+            out_shape=jax.ShapeDtypeStruct((halved, shard, SUB, LANES), f32),
+            scratch_shapes=[per_mode, per_mode],
+            compiler_params=wide,
+            cost_estimate=pl.CostEstimate(flops=2**24, bytes_accessed=2**21, transcendentals=0),
+            name="local",
+        )(u_t, rate, residue, skip.reshape(parts, GROUPS, LANES))
+
+    near = [local(0, decay_rate)]
+    got, near[0] = lax.optimization_barrier((got, near[0]))
     back = pl.pallas_call(
         lambda *refs: owner_kernel(width, shard, steps, *refs),
-        out_shape=jax.ShapeDtypeStruct((devices, 2 * SUB, LANES), f32),
+        out_shape=jax.ShapeDtypeStruct((devices, 5, 2, LANES), jnp.bfloat16),
         compiler_params=limit,
         name="owner",
     )(got, decay_rate, residue, skip)
 
+    back, rate = lax.optimization_barrier((back, decay_rate))
     given = lax.all_to_all(back, "seq", split_axis=0, concat_axis=0, tiled=True)
-
+    near.append(local(halved, rate))
+    given, near[1] = lax.optimization_barrier((given, near[1]))
+
+    def trade(x, pairs):
+        return lax.ppermute(x, "chan", pairs + [(b, a) for a, b in pairs])
+
+    tile = jax.ShapeDtypeStruct((SUB, LANES), f32)
     partial = pl.pallas_call(
-        lambda *refs: decode_kernel(steps, *refs),
+        decode_kernel,
         grid=(1,),
         in_specs=[
-            pl.BlockSpec((devices, SUB, LANES), lambda i: (0, 1, 0)),
+            pl.BlockSpec((devices, 1, 2, LANES), lambda i: (0, 4, 0, 0)),
             pl.BlockSpec((chans, LANES), lambda i: (0, 0)),
         ],
-        out_specs=pl.BlockSpec((4, batch, LANES), lambda i: (0, 0, 0)),
-        out_shape=jax.ShapeDtypeStruct((4, batch, LANES), f32),
+        out_specs=pl.BlockSpec((SUB, LANES), lambda i: (0, 0)),
+        out_shape=tile,
         compiler_params=limit,
         name="decode",
     )(given, out_weight)
-    pieces = lax.all_to_all(partial, "chan", split_axis=0, concat_axis=0, tiled=True)
-
-    mixed = pl.pallas_call(
-        lambda *refs: last_kernel(modes, shard, *refs),
-        grid=(parts,),
-        in_specs=[
-            pl.BlockSpec((devices // parts, SUB, LANES), lambda h: (h, 0, 0)),
-            in_time,
-            pl.BlockSpec((1, batch, block, shard), lambda h: (0, 0, h, 0)),
-            by_part,
-            by_part,
-        ],
-        out_specs=pl.BlockSpec((batch, block, shard), lambda h: (0, h, 0)),
-        out_shape=jax.ShapeDtypeStruct((batch, chans, shard), jnp.bfloat16),
-        scratch_shapes=[across, per_mode, per_mode, per_mode],
-        compiler_params=wide,
-        cost_estimate=pl.CostEstimate(flops=2**25, bytes_accessed=2**22, transcendentals=0),
-        name="last",
-    )(given, near, features, decay_rate, residue)
+    other = trade(partial, [(0, 1), (2, 3)])
+
+    def last(first, count, rate, *made):
+        shifted = pl.BlockSpec((modes, block), lambda h: (0, h + first))
+        return pl.pallas_call(
+            lambda *refs: last_kernel(modes, shard, *refs),
+            grid=(count,),
+            in_specs=[
+                pl.BlockSpec((devices // parts, 4, 2, LANES), lambda h: (h + first, 0, 0, 0)),
+                in_time,
+                pl.BlockSpec((1, batch, block, shard), lambda h: (0, 0, h + first, 0)),
+                shifted,
+                shifted,
+            ] + [pl.BlockSpec(memory_space=pl.ANY)] * len(made),
+            out_specs=pl.BlockSpec((batch, block, shard), lambda h: (0, h + first, 0)),
+            out_shape=jax.ShapeDtypeStruct((batch, chans, shard), jnp.bfloat16),
+            scratch_shapes=[across, per_mode, per_mode, per_mode],
+            input_output_aliases={5: 0} if made else {},
+            compiler_params=wide,
+            cost_estimate=pl.CostEstimate(flops=2**24, bytes_accessed=2**21, transcendentals=0),
+            name="last",
+        )(given, near[first // count], features, rate, residue, *made)
+
+    mixed = last(0, parts // 2, decay_rate)
+    other, mixed = lax.optimization_barrier((other, mixed))
+    pair = pl.pallas_call(add_kernel, out_shape=tile, compiler_params=limit, name="add")(partial, other)
+    pair, rate = lax.optimization_barrier((pair, decay_rate))
+    other = trade(pair, [(0, 3), (1, 2)])
+    mixed = last(parts // 2, parts // 2, rate, mixed)
 
     decoded = pl.pallas_call(
         lambda *refs: finish_kernel(steps, *refs),
         out_shape=jax.ShapeDtypeStruct((batch, steps, 32), jnp.bfloat16),
         compiler_params=limit,
         name="finish",
-    )(pieces)
+    )(pair, other)
     return (mixed, decoded)
 
 

time: 63.8 us -> 58.5 us (0.917)
  blocking collectives: 16.7 us -> 0 us
  waiting for transfers between devices: 4.74 us -> 9.01 us
  starting transfers between devices: 17.6 us -> 21.4 us
  Pallas kernels: 23.6 us -> 27 us
    all_to_all x1 -> x0, blocking collectives: 16.7 us -> none  [body(): given = lax.all_to_all(back, 'seq', split_axis=0, concat_axis=0, tiled=True)]
    ppermute x0 -> x2, starting transfers between devices: none -> 6.44 us  [trade(): return lax.ppermute(x, 'chan', pairs + [(b, a) for a, b in pairs])]
    all_to_all x1, waiting for transfers between devices: 0.4 us -> 4.08 us  [body(): given = lax.all_to_all(back, 'seq', split_axis=0, concat_axis=0, tiled=True)]
    all_to_all x1, starting transfers between devices: 7.28 us -> 4.48 us  [body(): given = lax.all_to_all(back, 'seq', split_axis=0, concat_axis=0, tiled=True)]
    pallas_call x3 -> x6, Pallas kernels: 14.9 us -> 17.7 us  [the longest x2 9.58 us: local(): pl.pallas_call(lambda *refs: local_kernel(modes, shard, *refs), grid=(hal...]
    pallas_call x1, Pallas kernels: 0.47 us -> 1.22 us  [body(): pl.pallas_call(lambda *refs: owner_kernel(width, shard, steps, *refs), ou...]
  transfers between devices with their start and end apart: 2 -> 4, of which waited for: 2 -> 2; matrix products, arithmetic and copies ran while one was open for 0% -> 0% of each run, Pallas kernels for 22% -> 30%
where the time goes in v3:
time: 58.5 us; the launch traced here: 58.1 us
  Pallas kernels  27 us (46%)
  starting transfers between devices  21.4 us (37%)
  waiting for transfers between devices  9.01 us (15%)
  between operations  0.69 us (1%)
    all_to_all x1, starting transfers between devices, body(): got = lax.all_to_all(send, 'seq', split_axis=0, concat_axis=0, tiled=True)  10.5 us
    pallas_call x2, Pallas kernels, local(): pl.pallas_call(lambda *refs: local_kernel(modes, shard, *refs), grid=(hal...  9.58 us
    pallas_call x2, Pallas kernels, last(): pl.pallas_call(lambda *refs: last_kernel(modes, shard, *refs), grid=(coun...  7.75 us
    pallas_call x1, Pallas kernels, body(): pl.pallas_call(lambda *refs: first_kernel(modes, shard, *refs), grid_spec...  7.42 us
    ppermute x2, starting transfers between devices, trade(): return lax.ppermute(x, 'chan', pairs + [(b, a) for a, b in pairs])  6.44 us
    all_to_all x1, waiting for transfers between devices, body(): got = lax.all_to_all(send, 'seq', split_axis=0, concat_axis=0, tiled=True)  4.92 us
    all_to_all x1, starting transfers between devices, body(): given = lax.all_to_all(back, 'seq', split_axis=0, concat_axis=0, tiled=True)  4.48 us
    all_to_all x1, waiting for transfers between devices, body(): given = lax.all_to_all(back, 'seq', split_axis=0, concat_axis=0, tiled=True)  4.08 us
  transfers between devices with their start and end apart: 4, of which 2 were waited for; matrix products, arithmetic and copies ran while one was open for 0% of the time, Pallas kernels for 30%

profile of v3, /device:TPU:1, one launch (start us, length us, event | category | flops | bytes accessed | tf_op | source)
XLA Modules:
  0.0 58.1 jit_solution(775247688952955231)
XLA Ops:
  0.6 7.4 %first.1 = (f32[4,128,8,128]{3,2,1,0:T(8,128)}, bf16[64,16,128]{2,1,0:T(8,128)(2,1)}) custom-call(s32[2,4]{1,0:T(2,128)} %refs_0_.1, s32[2]{0:T(128)} %refs_1_.3, bf16[3,2,2048,128]{3,2,1,0:T(8,128)(2,1)} %refs_2_.11, bf16[3,2,2048,128]{3,2,1,0:T(8,128)(2,1)} %refs_2_.11, f32[16,2048]{1,0:T(8,128)} %refs_3_.4, bf16[512,128]{1,0:T(8,128)(2,1)} %refs_5_.1, ...), custom_call_target="tpu_custom_call" | custom-call | tf_op jit(solution)/shard_map/first/pallas_call | solution.py:257
  8.1 0.0 copy-start
  8.1 0.0 copy-start.4
  8.1 10.5 %all-to-all-start = ((bf16[64,16,128]{2,1,0:T(8,128)(2,1)}), bf16[64,16,128]{2,1,0:T(8,128)(2,1)S(1)}, u32[]{:S(2)}, u32[]{:S(2)}) async-start(bf16[64,16,128]{2,1,0:T(8,128)(2,1)} %get-tuple-element.14), calls=%async_computation | async-start | bytes 524288 | tf_op jit(solution)/shard_map/all_to_all | solution.py:281
  18.6 4.8 %local.2.refs_1_ = f32[2,128,8,128]{3,2,1,0:T(8,128)} custom-call(f32[4,128,8,128]{3,2,1,0:T(8,128)} %get-tuple-element.15.refs_0_, f32[16,2048]{1,0:T(8,128)} %refs_3_.4, f32[16,2048]{1,0:T(8,128)} %refs_4_.5, f32[4,4,128]{2,1,0:T(4,128)} %bitcast.3), custom_call_target="tpu_custom_call" | custom-call | flops 16777216 | bytes 2097152 | tf_op jit(solution)/shard_map/local/pallas_call | solution.py:287
  23.3 4.9 %all-to-all-done.refs_0_ = bf16[64,16,128]{2,1,0:T(8,128)(2,1)S(1)} async-done(((bf16[64,16,128]{2,1,0:T(8,128)(2,1)}), bf16[64,16,128]{2,1,0:T(8,128)(2,1)S(1)}, u32[]{:S(2)}, u32[]{:S(2)}) %all-to-all-start) | async-done | bytes 262176 | tf_op jit(solution)/shard_map/all_to_all | solution.py:281
  28.3 0.0 copy-done
  28.3 0.0 copy-done.1
  28.3 0.0 copy-done.4
  28.3 0.0 copy-start.3
  28.3 1.2 %owner.1 = bf16[64,5,2,128]{3,2,1,0:T(2,128)(2,1)} custom-call(bf16[64,16,128]{2,1,0:T(8,128)(2,1)S(1)} %all-to-all-done.refs_0_, f32[16,2048]{1,0:T(8,128)S(1)} %copy-done, f32[16,2048]{1,0:T(8,128)S(1)} %copy-done.1, f32[16,128]{1,0:T(8,128)S(1)} %bitcast.5), custom_call_target="tpu_custom_call" | custom-call | tf_op jit(solution)/shard_map/owner/pallas_call | solution.py:306
  29.5 4.5 %all-to-all-start.1 = ((bf16[64,5,2,128]{3,2,1,0:T(2,128)(2,1)}), bf16[64,5,2,128]{3,2,1,0:T(2,128)(2,1)S(1)}, u32[]{:S(2)}, u32[]{:S(2)}) async-start(bf16[64,5,2,128]{3,2,1,0:T(2,128)(2,1)} %owner.1), calls=%async_computation.1 | async-start | bytes 327680 | tf_op jit(solution)/shard_map/all_to_all | solution.py:314
  34.0 4.8 %local.3.refs_1_ = f32[2,128,8,128]{3,2,1,0:T(8,128)} custom-call(f32[4,128,8,128]{3,2,1,0:T(8,128)} %get-tuple-element.15.refs_0_, f32[16,2048]{1,0:T(8,128)} %refs_3_.4, f32[16,2048]{1,0:T(8,128)} %refs_4_.5, f32[4,4,128]{2,1,0:T(4,128)} %bitcast.4), custom_call_target="tpu_custom_call" | custom-call | flops 16777216 | bytes 2097152 | tf_op jit(solution)/shard_map/local/pallas_call | solution.py:287
  38.8 4.1 %all-to-all-done.1.mix_ref.refs_0_ = bf16[64,5,2,128]{3,2,1,0:T(2,128)(2,1)S(1)} async-done(((bf16[64,5,2,128]{3,2,1,0:T(2,128)(2,1)}), bf16[64,5,2,128]{3,2,1,0:T(2,128)(2,1)S(1)}, u32[]{:S(2)}, u32[]{:S(2)}) %all-to-all-start.1) | async-done | bytes 163872 | tf_op jit(solution)/shard_map/all_to_all | solution.py:314
  42.9 0.0 copy-done.3
  42.9 0.4 decode.1.a
  43.2 3.1 %collective-permute-start = (f32[8,128]{1,0:T(8,128)S(1)}, f32[8,128]{1,0:T(8,128)S(1)}, u32[]{:S(2)}, u32[]{:S(2)}) collective-permute-start(f32[8,128]{1,0:T(8,128)S(1)} %decode.1.a), channel_id=1, source_target_pairs={{0,1},{2,3},{1,0},{3,2},{4,5},{6,7},{5,4},{7,6},{8,9},{10,11},{9,8... | collective-permute-start | bytes 12296 | tf_op jit(solution)/shard_map/ppermute | solution.py:319
  46.3 0.0 copy-done.2
  46.3 3.9 %last.2.refs_5_ = bf16[2,2048,128]{2,1,0:T(8,128)(2,1)} custom-call(bf16[64,5,2,128]{3,2,1,0:T(2,128)(2,1)} %copy-done.2, f32[2,128,8,128]{3,2,1,0:T(8,128)} %local.2.refs_1_, bf16[3,2,2048,128]{3,2,1,0:T(8,128)(2,1)} %refs_2_.11, f32[16,2048]{1,0:T(8,128)} %refs_3_.4, f32[16,2048]{1,0:T(8,128)} %refs_4_.5), custom_call_target="tpu_custom_call" | custom-call | flops 16777216 | bytes 2097152 | tf_op jit(solution)/shard_map/last/pallas_call | solution.py:338
  50.2 0.0 collective-permute-done.b
  50.2 3.4 %collective-permute-start.1 = (f32[8,128]{1,0:T(8,128)S(1)}, f32[8,128]{1,0:T(8,128)S(1)}, u32[]{:S(2)}, u32[]{:S(2)}) collective-permute-start(f32[8,128]{1,0:T(8,128)S(1)} %add.1.refs_0_), channel_id=1, source_target_pairs={{0,3},{1,2},{3,0},{2,1},{4,7},{5,6},{7,4},{6,5},{8,11},{9,10},{11,... | collective-permute-start | bytes 12296 | tf_op jit(solution)/shard_map/ppermute | solution.py:319
  53.6 3.9 %last.3 = bf16[2,2048,128]{2,1,0:T(8,128)(2,1)} custom-call(bf16[64,5,2,128]{3,2,1,0:T(2,128)(2,1)} %copy-done.2, f32[2,128,8,128]{3,2,1,0:T(8,128)} %local.3.refs_1_, bf16[3,2,2048,128]{3,2,1,0:T(8,128)(2,1)} %refs_2_.11, f32[16,2048]{1,0:T(8,128)} %refs_3_.4, f32[16,2048]{1,0:T(8,128)} %refs_4_.5, ...), custom_call_target="tpu_custom_call", output_to_operand_aliasing={{}: (5, {})} | custom-call | flops 16777216 | bytes 2097152 | tf_op jit(solution)/shard_map/last/pallas_call | solution.py:338
  57.4 0.0 collective-permute-done.1.refs_1_
  57.4 0.7 %finish.1 = bf16[2,4,32]{2,1,0:T(4,128)(2,1)} custom-call(f32[8,128]{1,0:T(8,128)S(1)} %add.1.refs_0_, f32[8,128]{1,0:T(8,128)S(1)} %collective-permute-done.1.refs_1_), custom_call_target="tpu_custom_call" | custom-call | tf_op jit(solution)/shard_map/finish/pallas_call | solution.py:364
  (3 shorter events, 0.0 us)
Async XLA Ops:
  8.1 20.2 %copy-start = (f32[16,2048]{1,0:T(8,128)S(1)}, f32[16,2048]{1,0:T(8,128)}, u32[]{:S(2)}) copy-start(f32[16,2048]{1,0:T(8,128)} %refs_3_.4) | copy-start | bytes 393220
  8.1 20.2 %copy-start.1 = (f32[16,2048]{1,0:T(8,128)S(1)}, f32[16,2048]{1,0:T(8,128)}, u32[]{:S(2)}) copy-start(f32[16,2048]{1,0:T(8,128)} %refs_4_.5) | copy-start | bytes 393220
  8.1 20.2 %copy-start.4 = (f32[2048]{0:T(1024)S(1)}, f32[2048]{0:T(1024)}, u32[]{:S(2)}) copy-start(f32[2048]{0:T(1024)} %param.15) | copy-start | bytes 24580
  8.1 20.2 %all-to-all-start = ((bf16[64,16,128]{2,1,0:T(8,128)(2,1)}), bf16[64,16,128]{2,1,0:T(8,128)(2,1)S(1)}, u32[]{:S(2)}, u32[]{:S(2)}) async-start(bf16[64,16,128]{2,1,0:T(8,128)(2,1)} %get-tuple-element.14), calls=%async_computation | async-start | bytes 524288 | tf_op jit(solution)/shard_map/all_to_all | solution.py:281
  28.3 14.6 %copy-start.3 = (bf16[2048,128]{1,0:T(8,128)(2,1)S(1)}, bf16[2048,128]{1,0:T(8,128)(2,1)}, u32[]{:S(2)}) copy-start(bf16[2048,128]{1,0:T(8,128)(2,1)} %w_ref.1) | copy-start | bytes 1572868
  29.5 13.4 %all-to-all-start.1 = ((bf16[64,5,2,128]{3,2,1,0:T(2,128)(2,1)}), bf16[64,5,2,128]{3,2,1,0:T(2,128)(2,1)S(1)}, u32[]{:S(2)}, u32[]{:S(2)}) async-start(bf16[64,5,2,128]{3,2,1,0:T(2,128)(2,1)} %owner.1), calls=%async_computation.1 | async-start | bytes 327680 | tf_op jit(solution)/shard_map/all_to_all | solution.py:314
  42.9 3.4 %copy-start.2 = (bf16[64,5,2,128]{3,2,1,0:T(2,128)(2,1)}, bf16[64,5,2,128]{3,2,1,0:T(2,128)(2,1)S(1)}, u32[]{:S(2)}) copy-start(bf16[64,5,2,128]{3,2,1,0:T(2,128)(2,1)S(1)} %all-to-all-done.1.mix_ref.refs_0_) | copy-start | bytes 491524
  43.2 6.9 %collective-permute-start = (f32[8,128]{1,0:T(8,128)S(1)}, f32[8,128]{1,0:T(8,128)S(1)}, u32[]{:S(2)}, u32[]{:S(2)}) collective-permute-start(f32[8,128]{1,0:T(8,128)S(1)} %decode.1.a), channel_id=1, source_target_pairs={{0,1},{2,3},{1,0},{3,2},{4,5},{6,7},{5,4},{7,6},{8,9},{10,11},{9,8... | collective-permute-start | bytes 12296 | tf_op jit(solution)/shard_map/ppermute | solution.py:319
  50.2 7.3 %collective-permute-start.1 = (f32[8,128]{1,0:T(8,128)S(1)}, f32[8,128]{1,0:T(8,128)S(1)}, u32[]{:S(2)}, u32[]{:S(2)}) collective-permute-start(f32[8,128]{1,0:T(8,128)S(1)} %add.1.refs_0_), channel_id=1, source_target_pairs={{0,3},{1,2},{3,0},{2,1},{4,7},{5,6},{7,4},{6,5},{8,11},{9,10},{11,... | collective-permute-start | bytes 12296 | tf_op jit(solution)/shard_map/ppermute | solution.py:319

commit v4 on v3

--- a/solution.py
+++ b/solution.py
@@ -13,6 +13,7 @@
 EPS = 1e-05
 VMEM_LIMIT = 8 * 2**20
 WIDE_LIMIT = 60 * 2**20
+LAST_LIMIT = 50 * 2**20
 
 
 def quarter_of(shape):
@@ -79,12 +80,12 @@
         x16[...] = jnp.concatenate([high, scaled - high], axis=0).astype(jnp.bfloat16)
 
     fill(decay, rate_ref, batch, lambda x: jnp.exp(-x))
-    for g in range(GROUPS):
-        for b in range(batch):
+    for b in range(batch):
+        live = (position >= offsets[b]).astype(jnp.float32).astype(jnp.bfloat16) > 0
+        for g in range(GROUPS):
             rows = slice(g * LANES, (g + 1) * LANES)
-            product = k_ref[0, b, rows].astype(jnp.float32) * v_ref[0, b, rows].astype(jnp.float32)
-            u = rounded(jnp.where(position >= offsets[b], product, 0.0))
-            trans[pl.ds((b * GROUPS + g) * PITCH, shard), :] = u.T
+            u = jnp.where(live, k_ref[0, b, rows] * v_ref[0, b, rows], jnp.bfloat16(0))
+            trans[pl.ds((b * GROUPS + g) * PITCH, shard), :] = u.astype(jnp.float32).T
 
     terms = []
     for i in range(3):
@@ -113,11 +114,15 @@
             send[g * 4 + q] = jnp.concatenate([tile, sums[g * 4 + q]], axis=0).astype(jnp.bfloat16)
 
 
-def local_kernel(modes, shard, u_ref, rate_ref, res_ref, skip_ref, out, decay, weight):
+def local_kernel(modes, shard, u_ref, rate_ref, res_ref, skip_ref, q_ref, out, rate_out, gain_out, q_out, decay, weight):
     batch = SUB // GROUPS
     fill(decay, rate_ref, batch, lambda x: jnp.exp(-x))
     fill(weight, res_ref, batch, lambda x: x)
     rates, weights = tiles_of(decay, modes), tiles_of(weight, modes)
+    q_out[...] = q_ref[...]
+    for m in range(modes):
+        rate_out[0, m] = rates[m]
+        gain_out[0, m] = rates[m] * weights[m]
     skip = jnp.concatenate([skip_ref[0]] * batch, axis=0)
 
     def step(t, held):
@@ -210,23 +215,21 @@
         out[:, s, :] = total[s * rows:(s + 1) * rows, :32].astype(jnp.bfloat16)
 
 
-def last_kernel(modes, shard, carry_ref, near_ref, q_ref, rate_ref, res_ref, *rest):
-    out, trans, decay, weight, state = rest[-5:]
+def last_kernel(modes, shard, carry_ref, near_ref, rate_ref, gain_ref, q_ref, *rest):
+    out, trans, state = rest[-3:]
     batch = q_ref.shape[1]
-    fill(decay, rate_ref, batch, lambda x: jnp.exp(-x))
-    fill(weight, res_ref, batch, lambda x: x)
     for g in range(GROUPS):
-        tiles = [jnp.concatenate([carry_ref[g * 4 + q, n].astype(jnp.float32) for n in range(4)], axis=0) for q in range(4)]
+        tiles = [carry_ref[g * 4 + q].astype(jnp.float32).reshape(SUB, LANES) for q in range(4)]
         tiles = spread(tiles)
         for r in range(4):
             state[pl.ds((r // 2) * GROUPS + g + (r % 2) * SUB * PAD, SUB, stride=PAD), :] = tiles[r]
-    rates, weights = tiles_of(decay, modes), tiles_of(weight, modes)
+    rates = [rate_ref[0, m] for m in range(modes)]
 
     def step(t, held):
         trans[pl.ds(t, SUB, stride=PITCH), :] = pairs_sum(list(held) + [near_ref[0, t]])
         return tuple(rates[m] * held[m] for m in range(modes))
 
-    held = tuple(weights[m] * (rates[m] * state[m * PAD:m * PAD + SUB, :]) for m in range(modes))
+    held = tuple(gain_ref[0, m] * state[m * PAD:m * PAD + SUB, :] for m in range(modes))
     lax.fori_loop(0, shard, step, held, unroll=4)
     for b in range(batch):
         for g in range(GROUPS):
@@ -281,6 +284,8 @@
     got = lax.all_to_all(send, "seq", split_axis=0, concat_axis=0, tiled=True)
 
     halved = parts // 2
+    own = pl.BlockSpec((1, batch, block, shard), lambda h: (h, 0, 0, 0))
+    tiles = pl.BlockSpec((1, modes, SUB, LANES), lambda h: (h, 0, 0, 0))
 
     def local(first, rate):
         shifted = pl.BlockSpec((modes, block), lambda h: (0, h + first))
@@ -292,17 +297,23 @@
                 shifted,
                 shifted,
                 pl.BlockSpec((1, GROUPS, LANES), lambda h: (h + first, 0, 0)),
+                pl.BlockSpec((1, batch, block, shard), lambda h: (0, 0, h + first, 0)),
             ],
-            out_specs=in_time,
-            out_shape=jax.ShapeDtypeStruct((halved, shard, SUB, LANES), f32),
+            out_specs=[in_time, tiles, tiles, own],
+            out_shape=[
+                jax.ShapeDtypeStruct((halved, shard, SUB, LANES), f32),
+                jax.ShapeDtypeStruct((halved, modes, SUB, LANES), f32),
+                jax.ShapeDtypeStruct((halved, modes, SUB, LANES), f32),
+                jax.ShapeDtypeStruct((halved, batch, block, shard), jnp.bfloat16),
+            ],
             scratch_shapes=[per_mode, per_mode],
             compiler_params=wide,
             cost_estimate=pl.CostEstimate(flops=2**24, bytes_accessed=2**21, transcendentals=0),
             name="local",
-        )(u_t, rate, residue, skip.reshape(parts, GROUPS, LANES))
+        )(u_t, rate, residue, skip.reshape(parts, GROUPS, LANES), features)
 
     near = [local(0, decay_rate)]
-    got, near[0] = lax.optimization_barrier((got, near[0]))
+    got, near[0] = lax.optimization_barrier((got, tuple(near[0])))
     back = pl.pallas_call(
         lambda *refs: owner_kernel(width, shard, steps, *refs),
         out_shape=jax.ShapeDtypeStruct((devices, 5, 2, LANES), jnp.bfloat16),
@@ -313,7 +324,7 @@
     back, rate = lax.optimization_barrier((back, decay_rate))
     given = lax.all_to_all(back, "seq", split_axis=0, concat_axis=0, tiled=True)
     near.append(local(halved, rate))
-    given, near[1] = lax.optimization_barrier((given, near[1]))
+    given, near[1] = lax.optimization_barrier((given, tuple(near[1])))
 
     def trade(x, pairs):
         return lax.ppermute(x, "chan", pairs + [(b, a) for a, b in pairs])
@@ -333,33 +344,32 @@
     )(given, out_weight)
     other = trade(partial, [(0, 1), (2, 3)])
 
-    def last(first, count, rate, *made):
-        shifted = pl.BlockSpec((modes, block), lambda h: (0, h + first))
+    def last(first, mine, *made):
         return pl.pallas_call(
             lambda *refs: last_kernel(modes, shard, *refs),
-            grid=(count,),
+            grid=(halved,),
             in_specs=[
                 pl.BlockSpec((devices // parts, 4, 2, LANES), lambda h: (h + first, 0, 0, 0)),
                 in_time,
-                pl.BlockSpec((1, batch, block, shard), lambda h: (0, 0, h + first, 0)),
-                shifted,
-                shifted,
+                tiles,
+                tiles,
+                own,
             ] + [pl.BlockSpec(memory_space=pl.ANY)] * len(made),
             out_specs=pl.BlockSpec((batch, block, shard), lambda h: (0, h + first, 0)),
             out_shape=jax.ShapeDtypeStruct((batch, chans, shard), jnp.bfloat16),
-            scratch_shapes=[across, per_mode, per_mode, per_mode],
+            scratch_shapes=[across, per_mode],
             input_output_aliases={5: 0} if made else {},
-            compiler_params=wide,
+            compiler_params=pltpu.CompilerParams(vmem_limit_bytes=LAST_LIMIT),
             cost_estimate=pl.CostEstimate(flops=2**24, bytes_accessed=2**21, transcendentals=0),
             name="last",
-        )(given, near[first // count], features, rate, residue, *made)
-
-    mixed = last(0, parts // 2, decay_rate)
+        )(given, *mine, *made)
+
+    mixed = last(0, near[0])
     other, mixed = lax.optimization_barrier((other, mixed))
     pair = pl.pallas_call(add_kernel, out_shape=tile, compiler_params=limit, name="add")(partial, other)
-    pair, rate = lax.optimization_barrier((pair, decay_rate))
+    pair, second = lax.optimization_barrier((pair, tuple(near[1])))
     other = trade(pair, [(0, 3), (1, 2)])
-    mixed = last(parts // 2, parts // 2, rate, mixed)
+    mixed = last(halved, second, mixed)
 
     decoded = pl.pallas_call(
         lambda *refs: finish_kernel(steps, *refs),

time: 58.5 us -> 56.9 us (0.973)
  Pallas kernels: 27 us -> 25.5 us
  local copies, waits for them, and re-layouts: 0.02 us -> 0.96 us
  waiting for transfers between devices: 9.01 us -> 8.13 us
    pallas_call x2, Pallas kernels: 7.75 us -> 5.48 us  [last(): pl.pallas_call(lambda *refs: last_kernel(modes, shard, *refs), grid=(halv...]
    unnamed x10 -> x24, local copies, waits for them, and re-layouts: 0.02 us -> 0.96 us
    pallas_call x2, Pallas kernels: 9.58 us -> 10.4 us  [local(): pl.pallas_call(lambda *refs: local_kernel(modes, shard, *refs), grid=(hal...]
  transfers between devices with their start and end apart: 4 -> 4, of which waited for: 2 -> 2; matrix products, arithmetic and copies ran while one was open for 0% -> 0% of each run, Pallas kernels for 30% -> 28%
where the time goes in v4:
time: 56.9 us; the launch traced here: 56.5 us
  Pallas kernels  25.5 us (45%)
  starting transfers between devices  21.2 us (37%)
  waiting for transfers between devices  8.13 us (14%)
  local copies, waits for them, and re-layouts  0.96 us (2%)
  between operations  0.73 us (1%)
    pallas_call x2, Pallas kernels, local(): pl.pallas_call(lambda *refs: local_kernel(modes, shard, *refs), grid=(hal...  10.4 us
    all_to_all x1, starting transfers between devices, body(): got = lax.all_to_all(send, 'seq', split_axis=0, concat_axis=0, tiled=True)  10.3 us
    pallas_call x1, Pallas kernels, body(): pl.pallas_call(lambda *refs: first_kernel(modes, shard, *refs), grid_spec...  7.44 us
    ppermute x2, starting transfers between devices, trade(): return lax.ppermute(x, 'chan', pairs + [(b, a) for a, b in pairs])  6.35 us
    pallas_call x2, Pallas kernels, last(): pl.pallas_call(lambda *refs: last_kernel(modes, shard, *refs), grid=(halv...  5.48 us
    all_to_all x1, waiting for transfers between devices, body(): got = lax.all_to_all(send, 'seq', split_axis=0, concat_axis=0, tiled=True)  4.55 us
    all_to_all x1, starting transfers between devices, body(): given = lax.all_to_all(back, 'seq', split_axis=0, concat_axis=0, tiled=True)  4.48 us
    all_to_all x1, waiting for transfers between devices, body(): given = lax.all_to_all(back, 'seq', split_axis=0, concat_axis=0, tiled=True)  3.58 us
  transfers between devices with their start and end apart: 4, of which 2 were waited for; matrix products, arithmetic and copies ran while one was open for 0% of the time, Pallas kernels for 28%

profile of v4, /device:TPU:1, one launch (start us, length us, event | category | flops | bytes accessed | tf_op | source)
XLA Modules:
  0.0 56.5 jit_solution(10414588350726084712)
XLA Ops:
  0.6 7.4 %first.1 = (f32[4,128,8,128]{3,2,1,0:T(8,128)}, bf16[64,16,128]{2,1,0:T(8,128)(2,1)}) custom-call(s32[2,4]{1,0:T(2,128)} %refs_0_.1, s32[2]{0:T(128)} %refs_1_.3, bf16[3,2,2048,128]{3,2,1,0:T(8,128)(2,1)} %refs_4_.5, bf16[3,2,2048,128]{3,2,1,0:T(8,128)(2,1)} %refs_4_.5, f32[16,2048]{1,0:T(8,128)} %refs_1_.6, bf16[512,128]{1,0:T(8,128)(2,1)} %refs_5_.1, ...), custom_call_target="tpu_custom_call" | custom-call | tf_op jit(solution)/shard_map/first/pallas_call | solution.py:260
  8.1 10.3 %all-to-all-start = ((bf16[64,16,128]{2,1,0:T(8,128)(2,1)}), bf16[64,16,128]{2,1,0:T(8,128)(2,1)S(1)}, u32[]{:S(2)}, u32[]{:S(2)}) async-start(bf16[64,16,128]{2,1,0:T(8,128)(2,1)} %get-tuple-element.31), calls=%async_computation | async-start | bytes 524288 | tf_op jit(solution)/shard_map/all_to_all | solution.py:284
  18.4 0.0 copy-start
  18.4 0.0 copy-start.1
  18.4 0.0 copy-start.11
  18.5 5.1 %local.2 = (f32[2,128,8,128]{3,2,1,0:T(8,128)}, f32[2,16,8,128]{3,2,1,0:T(8,128)}, f32[2,16,8,128]{3,2,1,0:T(8,128)}, bf16[2,2,512,128]{3,2,1,0:T(8,128)(2,1)}) custom-call(f32[4,128,8,128]{3,2,1,0:T(8,128)} %get-tuple-element.32.refs_0_, f32[16,2048]{1,0:T(8,128)} %refs_1_.6, f32[16,2048]{1,0:T(8,128)} %refs_2_.7, f32[4,4,128]{2,1,0:T(4,128)} %bitcast.3, ...), custom_call_target="tpu_custom_call" | custom-call | flops 16777216 | bytes 2097152 | tf_op jit(solution)/shard_map/local/pallas_call | solution.py:292
  23.6 4.5 %all-to-all-done.refs_0_ = bf16[64,16,128]{2,1,0:T(8,128)(2,1)S(1)} async-done(((bf16[64,16,128]{2,1,0:T(8,128)(2,1)}), bf16[64,16,128]{2,1,0:T(8,128)(2,1)S(1)}, u32[]{:S(2)}, u32[]{:S(2)}) %all-to-all-start) | async-done | bytes 262176 | tf_op jit(solution)/shard_map/all_to_all | solution.py:284
  28.1 0.0 copy-done.1
  28.1 1.2 %owner.1 = bf16[64,5,2,128]{3,2,1,0:T(2,128)(2,1)} custom-call(bf16[64,16,128]{2,1,0:T(8,128)(2,1)S(1)} %all-to-all-done.refs_0_, f32[16,2048]{1,0:T(8,128)S(1)} %copy-done, f32[16,2048]{1,0:T(8,128)S(1)} %copy-done.1, f32[16,128]{1,0:T(8,128)S(1)} %bitcast.5), custom_call_target="tpu_custom_call" | custom-call | tf_op jit(solution)/shard_map/owner/pallas_call | solution.py:317
  29.4 4.5 %all-to-all-start.1 = ((bf16[64,5,2,128]{3,2,1,0:T(2,128)(2,1)}), bf16[64,5,2,128]{3,2,1,0:T(2,128)(2,1)S(1)}, u32[]{:S(2)}, u32[]{:S(2)}) async-start(bf16[64,5,2,128]{3,2,1,0:T(2,128)(2,1)} %owner.1), calls=%async_computation.1 | async-start | bytes 327680 | tf_op jit(solution)/shard_map/all_to_all | solution.py:325
  33.9 0.0 copy-start.4
  33.9 0.0 copy-start.2
  33.9 5.2 %local.3 = (f32[2,128,8,128]{3,2,1,0:T(8,128)}, f32[2,16,8,128]{3,2,1,0:T(8,128)}, f32[2,16,8,128]{3,2,1,0:T(8,128)}, bf16[2,2,512,128]{3,2,1,0:T(8,128)(2,1)}) custom-call(f32[4,128,8,128]{3,2,1,0:T(8,128)} %get-tuple-element.32.refs_0_, f32[16,2048]{1,0:T(8,128)} %refs_1_.6, f32[16,2048]{1,0:T(8,128)} %refs_2_.7, f32[4,4,128]{2,1,0:T(4,128)} %bitcast.4, ...), custom_call_target="tpu_custom_call" | custom-call | flops 16777216 | bytes 2097152 | tf_op jit(solution)/shard_map/local/pallas_call | solution.py:292
  39.1 3.6 %all-to-all-done.1.mix_ref.refs_0_ = bf16[64,5,2,128]{3,2,1,0:T(2,128)(2,1)S(1)} async-done(((bf16[64,5,2,128]{3,2,1,0:T(2,128)(2,1)}), bf16[64,5,2,128]{3,2,1,0:T(2,128)(2,1)S(1)}, u32[]{:S(2)}, u32[]{:S(2)}) %all-to-all-start.1) | async-done | bytes 163872 | tf_op jit(solution)/shard_map/all_to_all | solution.py:325
  42.7 0.0 copy-done.4
  42.7 0.4 decode.1.a
  43.1 3.0 %collective-permute-start = (f32[8,128]{1,0:T(8,128)S(1)}, f32[8,128]{1,0:T(8,128)S(1)}, u32[]{:S(2)}, u32[]{:S(2)}) collective-permute-start(f32[8,128]{1,0:T(8,128)S(1)} %decode.1.a), channel_id=1, source_target_pairs={{0,1},{2,3},{1,0},{3,2},{4,5},{6,7},{5,4},{7,6},{8,9},{10,11},{9,8... | collective-permute-start | bytes 12296 | tf_op jit(solution)/shard_map/ppermute | solution.py:330
  46.1 0.9 %copy-done.8 = f32[2,16,8,128]{3,2,1,0:T(8,128)S(1)} copy-done((f32[2,16,8,128]{3,2,1,0:T(8,128)S(1)}, f32[2,16,8,128]{3,2,1,0:T(8,128)}, u32[]{:S(2)}) %copy-start.8) | copy-done | bytes 131096
  47.0 2.7 %last.2.refs_5_ = bf16[2,2048,128]{2,1,0:T(8,128)(2,1)} custom-call(bf16[64,5,2,128]{3,2,1,0:T(2,128)(2,1)S(1)} %all-to-all-done.1.mix_ref.refs_0_, f32[2,128,8,128]{3,2,1,0:T(8,128)S(1)} %copy-done.2, f32[2,16,8,128]{3,2,1,0:T(8,128)S(1)} %copy-done.7, f32[2,16,8,128]{3,2,1,0:T(8,128)S(1)} %copy-done.8, bf16[2,2,512,128]{3,2,1,0:T(8,128)(2,1)S(1)} %copy-done.5), custom_call_target="tpu_custom_call" | custom-call | flops 16777216 | bytes 2097152 | tf_op jit(solution)/shard_map/last/pallas_call | solution.py:348
  49.8 0.0 collective-permute-done.b
  49.8 3.3 %collective-permute-start.1 = (f32[8,128]{1,0:T(8,128)S(1)}, f32[8,128]{1,0:T(8,128)S(1)}, u32[]{:S(2)}, u32[]{:S(2)}) collective-permute-start(f32[8,128]{1,0:T(8,128)S(1)} %add.1.refs_0_), channel_id=1, source_target_pairs={{0,3},{1,2},{3,0},{2,1},{4,7},{5,6},{7,4},{6,5},{8,11},{9,10},{11,... | collective-permute-start | bytes 12296 | tf_op jit(solution)/shard_map/ppermute | solution.py:330
  53.1 2.8 %last.3 = bf16[2,2048,128]{2,1,0:T(8,128)(2,1)} custom-call(bf16[64,5,2,128]{3,2,1,0:T(2,128)(2,1)S(1)} %all-to-all-done.1.mix_ref.refs_0_, f32[2,128,8,128]{3,2,1,0:T(8,128)S(1)} %copy-done.3, f32[2,16,8,128]{3,2,1,0:T(8,128)S(1)} %copy-done.9, f32[2,16,8,128]{3,2,1,0:T(8,128)S(1)} %copy-done.10, ...), custom_call_target="tpu_custom_call", output_to_operand_aliasing={{}: (5, {})} | custom-call | flops 16777216 | bytes 2097152 | tf_op jit(solution)/shard_map/last/pallas_call | solution.py:348
  55.8 0.0 collective-permute-done.1.refs_1_
  55.8 0.7 %finish.1 = bf16[2,4,32]{2,1,0:T(4,128)(2,1)} custom-call(f32[8,128]{1,0:T(8,128)S(1)} %add.1.refs_0_, f32[8,128]{1,0:T(8,128)S(1)} %collective-permute-done.1.refs_1_), custom_call_target="tpu_custom_call" | custom-call | tf_op jit(solution)/shard_map/finish/pallas_call | solution.py:374
  (17 shorter events, 0.0 us)
Async XLA Ops:
  8.1 20.0 %all-to-all-start = ((bf16[64,16,128]{2,1,0:T(8,128)(2,1)}), bf16[64,16,128]{2,1,0:T(8,128)(2,1)S(1)}, u32[]{:S(2)}, u32[]{:S(2)}) async-start(bf16[64,16,128]{2,1,0:T(8,128)(2,1)} %get-tuple-element.31), calls=%async_computation | async-start | bytes 524288 | tf_op jit(solution)/shard_map/all_to_all | solution.py:284
  18.4 9.7 %copy-start = (f32[16,2048]{1,0:T(8,128)S(1)}, f32[16,2048]{1,0:T(8,128)}, u32[]{:S(2)}) copy-start(f32[16,2048]{1,0:T(8,128)} %refs_1_.6) | copy-start | bytes 393220
  18.4 9.7 %copy-start.1 = (f32[16,2048]{1,0:T(8,128)S(1)}, f32[16,2048]{1,0:T(8,128)}, u32[]{:S(2)}) copy-start(f32[16,2048]{1,0:T(8,128)} %refs_2_.7) | copy-start | bytes 393220
  18.4 9.7 %copy-start.11 = (f32[2048]{0:T(1024)S(1)}, f32[2048]{0:T(1024)}, u32[]{:S(2)}) copy-start(f32[2048]{0:T(1024)} %param.15) | copy-start | bytes 24580
  29.4 13.4 %all-to-all-start.1 = ((bf16[64,5,2,128]{3,2,1,0:T(2,128)(2,1)}), bf16[64,5,2,128]{3,2,1,0:T(2,128)(2,1)S(1)}, u32[]{:S(2)}, u32[]{:S(2)}) async-start(bf16[64,5,2,128]{3,2,1,0:T(2,128)(2,1)} %owner.1), calls=%async_computation.1 | async-start | bytes 327680 | tf_op jit(solution)/shard_map/all_to_all | solution.py:325
  33.9 8.9 %copy-start.4 = (bf16[2048,128]{1,0:T(8,128)(2,1)S(1)}, bf16[2048,128]{1,0:T(8,128)(2,1)}, u32[]{:S(2)}) copy-start(bf16[2048,128]{1,0:T(8,128)(2,1)} %w_ref.1) | copy-start | bytes 1572868
  33.9 12.3 %copy-start.2 = (f32[2,128,8,128]{3,2,1,0:T(8,128)S(1)}, f32[2,128,8,128]{3,2,1,0:T(8,128)}, u32[]{:S(2)}) copy-start(f32[2,128,8,128]{3,2,1,0:T(8,128)} %get-tuple-element.45.refs_1_) | copy-start | bytes 3145732
  33.9 12.2 %copy-start.5 = (bf16[2,2,512,128]{3,2,1,0:T(8,128)(2,1)S(1)}, bf16[2,2,512,128]{3,2,1,0:T(8,128)(2,1)}, u32[]{:S(2)}) copy-start(bf16[2,2,512,128]{3,2,1,0:T(8,128)(2,1)} %get-tuple-element.48.refs_4_) | copy-start | bytes 1572868
  33.9 12.2 %copy-start.7 = (f32[2,16,8,128]{3,2,1,0:T(8,128)S(1)}, f32[2,16,8,128]{3,2,1,0:T(8,128)}, u32[]{:S(2)}) copy-start(f32[2,16,8,128]{3,2,1,0:T(8,128)} %get-tuple-element.46.refs_2_) | copy-start | bytes 393220
  39.1 13.9 %copy-start.3 = (f32[2,128,8,128]{3,2,1,0:T(8,128)S(1)}, f32[2,128,8,128]{3,2,1,0:T(8,128)}, u32[]{:S(2)}) copy-start(f32[2,128,8,128]{3,2,1,0:T(8,128)} %get-tuple-element.54.refs_1_) | copy-start | bytes 3145732
  42.7 10.4 %copy-start.6 = (bf16[2,2,512,128]{3,2,1,0:T(8,128)(2,1)S(1)}, bf16[2,2,512,128]{3,2,1,0:T(8,128)(2,1)}, u32[]{:S(2)}) copy-start(bf16[2,2,512,128]{3,2,1,0:T(8,128)(2,1)} %get-tuple-element.57.refs_4_) | copy-start | bytes 1572868
  43.1 6.7 %collective-permute-start = (f32[8,128]{1,0:T(8,128)S(1)}, f32[8,128]{1,0:T(8,128)S(1)}, u32[]{:S(2)}, u32[]{:S(2)}) collective-permute-start(f32[8,128]{1,0:T(8,128)S(1)} %decode.1.a), channel_id=1, source_target_pairs={{0,1},{2,3},{1,0},{3,2},{4,5},{6,7},{5,4},{7,6},{8,9},{10,11},{9,8... | collective-permute-start | bytes 12296 | tf_op jit(solution)/shard_map/ppermute | solution.py:330
  46.1 0.9 %copy-start.8 = (f32[2,16,8,128]{3,2,1,0:T(8,128)S(1)}, f32[2,16,8,128]{3,2,1,0:T(8,128)}, u32[]{:S(2)}) copy-start(f32[2,16,8,128]{3,2,1,0:T(8,128)} %get-tuple-element.47.refs_3_) | copy-start | bytes 393220
  47.0 6.1 %copy-start.9 = (f32[2,16,8,128]{3,2,1,0:T(8,128)S(1)}, f32[2,16,8,128]{3,2,1,0:T(8,128)}, u32[]{:S(2)}) copy-start(f32[2,16,8,128]{3,2,1,0:T(8,128)} %get-tuple-element.55.refs_2_) | copy-start | bytes 393220
  47.0 6.1 %copy-start.10 = (f32[2,16,8,128]{3,2,1,0:T(8,128)S(1)}, f32[2,16,8,128]{3,2,1,0:T(8,128)}, u32[]{:S(2)}) copy-start(f32[2,16,8,128]{3,2,1,0:T(8,128)} %get-tuple-element.56.refs_3_) | copy-start | bytes 393220
  49.8 6.1 %collective-permute-start.1 = (f32[8,128]{1,0:T(8,128)S(1)}, f32[8,128]{1,0:T(8,128)S(1)}, u32[]{:S(2)}, u32[]{:S(2)}) collective-permute-start(f32[8,128]{1,0:T(8,128)S(1)} %add.1.refs_0_), channel_id=1, source_target_pairs={{0,3},{1,2},{3,0},{2,1},{4,7},{5,6},{7,4},{6,5},{8,11},{9,10},{11,... | collective-permute-start | bytes 12296 | tf_op jit(solution)/shard_map/ppermute | solution.py:330

commit v5 on v4

--- a/solution.py
+++ b/solution.py
@@ -114,7 +114,7 @@
             send[g * 4 + q] = jnp.concatenate([tile, sums[g * 4 + q]], axis=0).astype(jnp.bfloat16)
 
 
-def local_kernel(modes, shard, u_ref, rate_ref, res_ref, skip_ref, q_ref, out, rate_out, gain_out, q_out, decay, weight):
+def local_kernel(modes, shard, u_ref, rate_ref, res_ref, skip_ref, q_ref, out, rate_out, q_out, decay, weight):
     batch = SUB // GROUPS
     fill(decay, rate_ref, batch, lambda x: jnp.exp(-x))
     fill(weight, res_ref, batch, lambda x: x)
@@ -122,7 +122,6 @@
     q_out[...] = q_ref[...]
     for m in range(modes):
         rate_out[0, m] = rates[m]
-        gain_out[0, m] = rates[m] * weights[m]
     skip = jnp.concatenate([skip_ref[0]] * batch, axis=0)
 
     def step(t, held):
@@ -159,11 +158,12 @@
     rate = packed(rate_ref)
     res = packed(res_ref)
     jump = jnp.exp(-rate * shard)
+    gain = res * jnp.exp(-rate)
     carried = jnp.zeros((SUB, LANES), jnp.float32)
     total = jnp.zeros((SUB, LANES), jnp.float32)
     for i in range(got.shape[0]):
         both = got[i].astype(jnp.float32)
-        sent = carried.astype(jnp.bfloat16)
+        sent = (gain * carried).astype(jnp.bfloat16)
         for n in range(4):
             back[i, n] = sent[2 * n:2 * n + 2]
         carried = jump * carried + both[:SUB]
@@ -215,7 +215,7 @@
         out[:, s, :] = total[s * rows:(s + 1) * rows, :32].astype(jnp.bfloat16)
 
 
-def last_kernel(modes, shard, carry_ref, near_ref, rate_ref, gain_ref, q_ref, *rest):
+def last_kernel(modes, shard, carry_ref, near_ref, rate_ref, q_ref, *rest):
     out, trans, state = rest[-3:]
     batch = q_ref.shape[1]
     for g in range(GROUPS):
@@ -229,7 +229,7 @@
         trans[pl.ds(t, SUB, stride=PITCH), :] = pairs_sum(list(held) + [near_ref[0, t]])
         return tuple(rates[m] * held[m] for m in range(modes))
 
-    held = tuple(gain_ref[0, m] * state[m * PAD:m * PAD + SUB, :] for m in range(modes))
+    held = tuple(state[m * PAD:m * PAD + SUB, :] for m in range(modes))
     lax.fori_loop(0, shard, step, held, unroll=4)
     for b in range(batch):
         for g in range(GROUPS):
@@ -299,10 +299,9 @@
                 pl.BlockSpec((1, GROUPS, LANES), lambda h: (h + first, 0, 0)),
                 pl.BlockSpec((1, batch, block, shard), lambda h: (0, 0, h + first, 0)),
             ],
-            out_specs=[in_time, tiles, tiles, own],
+            out_specs=[in_time, tiles, own],
             out_shape=[
                 jax.ShapeDtypeStruct((halved, shard, SUB, LANES), f32),
-                jax.ShapeDtypeStruct((halved, modes, SUB, LANES), f32),
                 jax.ShapeDtypeStruct((halved, modes, SUB, LANES), f32),
                 jax.ShapeDtypeStruct((halved, batch, block, shard), jnp.bfloat16),
             ],
@@ -352,13 +351,12 @@
                 pl.BlockSpec((devices // parts, 4, 2, LANES), lambda h: (h + first, 0, 0, 0)),
                 in_time,
                 tiles,
-                tiles,
                 own,
             ] + [pl.BlockSpec(memory_space=pl.ANY)] * len(made),
             out_specs=pl.BlockSpec((batch, block, shard), lambda h: (0, h + first, 0)),
             out_shape=jax.ShapeDtypeStruct((batch, chans, shard), jnp.bfloat16),
             scratch_shapes=[across, per_mode],
-            input_output_aliases={5: 0} if made else {},
+            input_output_aliases={4: 0} if made else {},
             compiler_params=pltpu.CompilerParams(vmem_limit_bytes=LAST_LIMIT),
             cost_estimate=pl.CostEstimate(flops=2**24, bytes_accessed=2**21, transcendentals=0),
             name="last",

time: 56.9 us -> 57.1 us (level)
  no operation moved by 1% of the time
where the time goes in v5:
time: 57.1 us; the launch traced here: 56.7 us
  Pallas kernels  25.5 us (45%)
  starting transfers between devices  21.2 us (37%)
  waiting for transfers between devices  8.24 us (14%)
  local copies, waits for them, and re-layouts  1.09 us (2%)
  between operations  0.71 us (1%)
    all_to_all x1, starting transfers between devices, body(): got = lax.all_to_all(send, 'seq', split_axis=0, concat_axis=0, tiled=True)  10.3 us
    pallas_call x2, Pallas kernels, local(): pl.pallas_call(lambda *refs: local_kernel(modes, shard, *refs), grid=(hal...  10.3 us
    pallas_call x1, Pallas kernels, body(): pl.pallas_call(lambda *refs: first_kernel(modes, shard, *refs), grid_spec...  7.45 us
    ppermute x2, starting transfers between devices, trade(): return lax.ppermute(x, 'chan', pairs + [(b, a) for a, b in pairs])  6.35 us
    pallas_call x2, Pallas kernels, last(): pl.pallas_call(lambda *refs: last_kernel(modes, shard, *refs), grid=(halv...  5.48 us
    all_to_all x1, waiting for transfers between devices, body(): got = lax.all_to_all(send, 'seq', split_axis=0, concat_axis=0, tiled=True)  4.58 us
    all_to_all x1, starting transfers between devices, body(): given = lax.all_to_all(back, 'seq', split_axis=0, concat_axis=0, tiled=True)  4.48 us
    all_to_all x1, waiting for transfers between devices, body(): given = lax.all_to_all(back, 'seq', split_axis=0, concat_axis=0, tiled=True)  3.66 us
  transfers between devices with their start and end apart: 4, of which 2 were waited for; matrix products, arithmetic and copies ran while one was open for 0% of the time, Pallas kernels for 28%

profile of v5, /device:TPU:1, one launch (start us, length us, event | category | flops | bytes accessed | tf_op | source)
XLA Modules:
  0.0 56.7 jit_solution(2482883143620678465)
XLA Ops:
  0.6 7.5 %first.1 = (f32[4,128,8,128]{3,2,1,0:T(8,128)}, bf16[64,16,128]{2,1,0:T(8,128)(2,1)}) custom-call(s32[2,4]{1,0:T(2,128)} %refs_0_.1, s32[2]{0:T(128)} %refs_1_.3, bf16[3,2,2048,128]{3,2,1,0:T(8,128)(2,1)} %refs_4_.5, bf16[3,2,2048,128]{3,2,1,0:T(8,128)(2,1)} %refs_4_.5, f32[16,2048]{1,0:T(8,128)} %refs_1_.6, bf16[512,128]{1,0:T(8,128)(2,1)} %refs_5_.1, ...), custom_call_target="tpu_custom_call" | custom-call | tf_op jit(solution)/shard_map/first/pallas_call | solution.py:260
  8.1 10.3 %all-to-all-start = ((bf16[64,16,128]{2,1,0:T(8,128)(2,1)}), bf16[64,16,128]{2,1,0:T(8,128)(2,1)S(1)}, u32[]{:S(2)}, u32[]{:S(2)}) async-start(bf16[64,16,128]{2,1,0:T(8,128)(2,1)} %get-tuple-element.26), calls=%async_computation | async-start | bytes 524288 | tf_op jit(solution)/shard_map/all_to_all | solution.py:284
  18.4 0.0 copy-start
  18.4 0.0 copy-start.1
  18.4 0.0 copy-start.9
  18.5 5.1 %local.2 = (f32[2,128,8,128]{3,2,1,0:T(8,128)}, f32[2,16,8,128]{3,2,1,0:T(8,128)}, bf16[2,2,512,128]{3,2,1,0:T(8,128)(2,1)}) custom-call(f32[4,128,8,128]{3,2,1,0:T(8,128)} %get-tuple-element.27.refs_0_, f32[16,2048]{1,0:T(8,128)} %refs_1_.6, f32[16,2048]{1,0:T(8,128)} %refs_2_.7, f32[4,4,128]{2,1,0:T(4,128)} %bitcast.3, bf16[3,2,2048,128]{3,2,1,0:T(8,128)(2,1)} %refs_4_.5), custom_call_target="tpu_custom_call" | custom-call | flops 16777216 | bytes 2097152 | tf_op jit(solution)/shard_map/local/pallas_call | solution.py:292
  23.6 4.6 %all-to-all-done.refs_0_ = bf16[64,16,128]{2,1,0:T(8,128)(2,1)S(1)} async-done(((bf16[64,16,128]{2,1,0:T(8,128)(2,1)}), bf16[64,16,128]{2,1,0:T(8,128)(2,1)S(1)}, u32[]{:S(2)}, u32[]{:S(2)}) %all-to-all-start) | async-done | bytes 262176 | tf_op jit(solution)/shard_map/all_to_all | solution.py:284
  28.1 0.0 copy-done.1
  28.1 1.2 %owner.1 = bf16[64,5,2,128]{3,2,1,0:T(2,128)(2,1)} custom-call(bf16[64,16,128]{2,1,0:T(8,128)(2,1)S(1)} %all-to-all-done.refs_0_, f32[16,2048]{1,0:T(8,128)S(1)} %copy-done, f32[16,2048]{1,0:T(8,128)S(1)} %copy-done.1, f32[16,128]{1,0:T(8,128)S(1)} %bitcast.5), custom_call_target="tpu_custom_call" | custom-call | tf_op jit(solution)/shard_map/owner/pallas_call | solution.py:316
  29.4 4.5 %all-to-all-start.1 = ((bf16[64,5,2,128]{3,2,1,0:T(2,128)(2,1)}), bf16[64,5,2,128]{3,2,1,0:T(2,128)(2,1)S(1)}, u32[]{:S(2)}, u32[]{:S(2)}) async-start(bf16[64,5,2,128]{3,2,1,0:T(2,128)(2,1)} %owner.1), calls=%async_computation.1 | async-start | bytes 327680 | tf_op jit(solution)/shard_map/all_to_all | solution.py:324
  33.9 0.0 copy-start.5
  33.9 0.0 copy-start.2
  33.9 5.2 %local.3 = (f32[2,128,8,128]{3,2,1,0:T(8,128)}, f32[2,16,8,128]{3,2,1,0:T(8,128)}, bf16[2,2,512,128]{3,2,1,0:T(8,128)(2,1)}) custom-call(f32[4,128,8,128]{3,2,1,0:T(8,128)} %get-tuple-element.27.refs_0_, f32[16,2048]{1,0:T(8,128)} %refs_1_.6, f32[16,2048]{1,0:T(8,128)} %refs_2_.7, f32[4,4,128]{2,1,0:T(4,128)} %bitcast.4, bf16[3,2,2048,128]{3,2,1,0:T(8,128)(2,1)} %refs_4_.5), custom_call_target="tpu_custom_call" | custom-call | flops 16777216 | bytes 2097152 | tf_op jit(solution)/shard_map/local/pallas_call | solution.py:292
  39.1 3.7 %all-to-all-done.1.mix_ref.refs_0_ = bf16[64,5,2,128]{3,2,1,0:T(2,128)(2,1)S(1)} async-done(((bf16[64,5,2,128]{3,2,1,0:T(2,128)(2,1)}), bf16[64,5,2,128]{3,2,1,0:T(2,128)(2,1)S(1)}, u32[]{:S(2)}, u32[]{:S(2)}) %all-to-all-start.1) | async-done | bytes 163872 | tf_op jit(solution)/shard_map/all_to_all | solution.py:324
  42.7 0.4 decode.1.a
  43.1 3.0 %collective-permute-start = (f32[8,128]{1,0:T(8,128)S(1)}, f32[8,128]{1,0:T(8,128)S(1)}, u32[]{:S(2)}, u32[]{:S(2)}) collective-permute-start(f32[8,128]{1,0:T(8,128)S(1)} %decode.1.a), channel_id=1, source_target_pairs={{0,1},{2,3},{1,0},{3,2},{4,5},{6,7},{5,4},{7,6},{8,9},{10,11},{9,8... | collective-permute-start | bytes 12296 | tf_op jit(solution)/shard_map/ppermute | solution.py:329
  46.2 0.0 copy-done.7
  46.2 1.0 %copy-done.6 = bf16[2,2,512,128]{3,2,1,0:T(8,128)(2,1)S(1)} copy-done((bf16[2,2,512,128]{3,2,1,0:T(8,128)(2,1)S(1)}, bf16[2,2,512,128]{3,2,1,0:T(8,128)(2,1)}, u32[]{:S(2)}) %copy-start.6) | copy-done | bytes 524312
  47.2 2.7 %last.2.refs_4_ = bf16[2,2048,128]{2,1,0:T(8,128)(2,1)} custom-call(bf16[64,5,2,128]{3,2,1,0:T(2,128)(2,1)S(1)} %all-to-all-done.1.mix_ref.refs_0_, f32[2,128,8,128]{3,2,1,0:T(8,128)S(1)} %copy-done.2, f32[2,16,8,128]{3,2,1,0:T(8,128)S(1)} %copy-done.7, bf16[2,2,512,128]{3,2,1,0:T(8,128)(2,1)S(1)} %copy-done.6), custom_call_target="tpu_custom_call" | custom-call | flops 16777216 | bytes 2097152 | tf_op jit(solution)/shard_map/last/pallas_call | solution.py:347
  49.9 0.0 collective-permute-done.b
  49.9 3.3 %collective-permute-start.1 = (f32[8,128]{1,0:T(8,128)S(1)}, f32[8,128]{1,0:T(8,128)S(1)}, u32[]{:S(2)}, u32[]{:S(2)}) collective-permute-start(f32[8,128]{1,0:T(8,128)S(1)} %add.1.refs_0_), channel_id=1, source_target_pairs={{0,3},{1,2},{3,0},{2,1},{4,7},{5,6},{7,4},{6,5},{8,11},{9,10},{11,... | collective-permute-start | bytes 12296 | tf_op jit(solution)/shard_map/ppermute | solution.py:329
  53.3 2.7 %last.3 = bf16[2,2048,128]{2,1,0:T(8,128)(2,1)} custom-call(bf16[64,5,2,128]{3,2,1,0:T(2,128)(2,1)S(1)} %all-to-all-done.1.mix_ref.refs_0_, f32[2,128,8,128]{3,2,1,0:T(8,128)S(1)} %copy-done.3, f32[2,16,8,128]{3,2,1,0:T(8,128)S(1)} %copy-done.8, bf16[2,2,512,128]{3,2,1,0:T(8,128)(2,1)S(1)} %copy-done.4, ...), custom_call_target="tpu_custom_call", output_to_operand_aliasing={{}: (4, {})} | custom-call | flops 16777216 | bytes 2097152 | tf_op jit(solution)/shard_map/last/pallas_call | solution.py:347
  56.0 0.0 collective-permute-done.1.refs_1_
  56.0 0.7 %finish.1 = bf16[2,4,32]{2,1,0:T(4,128)(2,1)} custom-call(f32[8,128]{1,0:T(8,128)S(1)} %add.1.refs_0_, f32[8,128]{1,0:T(8,128)S(1)} %collective-permute-done.1.refs_1_), custom_call_target="tpu_custom_call" | custom-call | tf_op jit(solution)/shard_map/finish/pallas_call | solution.py:372
  (13 shorter events, 0.0 us)
Async XLA Ops:
  8.1 20.0 %all-to-all-start = ((bf16[64,16,128]{2,1,0:T(8,128)(2,1)}), bf16[64,16,128]{2,1,0:T(8,128)(2,1)S(1)}, u32[]{:S(2)}, u32[]{:S(2)}) async-start(bf16[64,16,128]{2,1,0:T(8,128)(2,1)} %get-tuple-element.26), calls=%async_computation | async-start | bytes 524288 | tf_op jit(solution)/shard_map/all_to_all | solution.py:284
  18.4 9.7 %copy-start = (f32[16,2048]{1,0:T(8,128)S(1)}, f32[16,2048]{1,0:T(8,128)}, u32[]{:S(2)}) copy-start(f32[16,2048]{1,0:T(8,128)} %refs_1_.6) | copy-start | bytes 393220
  18.4 9.7 %copy-start.1 = (f32[16,2048]{1,0:T(8,128)S(1)}, f32[16,2048]{1,0:T(8,128)}, u32[]{:S(2)}) copy-start(f32[16,2048]{1,0:T(8,128)} %refs_2_.7) | copy-start | bytes 393220
  18.4 9.7 %copy-start.9 = (f32[2048]{0:T(1024)S(1)}, f32[2048]{0:T(1024)}, u32[]{:S(2)}) copy-start(f32[2048]{0:T(1024)} %param.15) | copy-start | bytes 24580
  29.4 13.4 %all-to-all-start.1 = ((bf16[64,5,2,128]{3,2,1,0:T(2,128)(2,1)}), bf16[64,5,2,128]{3,2,1,0:T(2,128)(2,1)S(1)}, u32[]{:S(2)}, u32[]{:S(2)}) async-start(bf16[64,5,2,128]{3,2,1,0:T(2,128)(2,1)} %owner.1), calls=%async_computation.1 | async-start | bytes 327680 | tf_op jit(solution)/shard_map/all_to_all | solution.py:324
  33.9 8.9 %copy-start.5 = (bf16[2048,128]{1,0:T(8,128)(2,1)S(1)}, bf16[2048,128]{1,0:T(8,128)(2,1)}, u32[]{:S(2)}) copy-start(bf16[2048,128]{1,0:T(8,128)(2,1)} %w_ref.1) | copy-start | bytes 1572868
  33.9 12.3 %copy-start.2 = (f32[2,128,8,128]{3,2,1,0:T(8,128)S(1)}, f32[2,128,8,128]{3,2,1,0:T(8,128)}, u32[]{:S(2)}) copy-start(f32[2,128,8,128]{3,2,1,0:T(8,128)} %get-tuple-element.38.refs_1_) | copy-start | bytes 3145732
  33.9 12.3 %copy-start.7 = (f32[2,16,8,128]{3,2,1,0:T(8,128)S(1)}, f32[2,16,8,128]{3,2,1,0:T(8,128)}, u32[]{:S(2)}) copy-start(f32[2,16,8,128]{3,2,1,0:T(8,128)} %get-tuple-element.39.refs_2_) | copy-start | bytes 393220
  39.1 14.2 %copy-start.3 = (f32[2,128,8,128]{3,2,1,0:T(8,128)S(1)}, f32[2,128,8,128]{3,2,1,0:T(8,128)}, u32[]{:S(2)}) copy-start(f32[2,128,8,128]{3,2,1,0:T(8,128)} %get-tuple-element.45.refs_1_) | copy-start | bytes 3145732
  39.1 14.2 %copy-start.4 = (bf16[2,2,512,128]{3,2,1,0:T(8,128)(2,1)S(1)}, bf16[2,2,512,128]{3,2,1,0:T(8,128)(2,1)}, u32[]{:S(2)}) copy-start(bf16[2,2,512,128]{3,2,1,0:T(8,128)(2,1)} %get-tuple-element.47.refs_3_) | copy-start | bytes 1572868
  43.1 6.8 %collective-permute-start = (f32[8,128]{1,0:T(8,128)S(1)}, f32[8,128]{1,0:T(8,128)S(1)}, u32[]{:S(2)}, u32[]{:S(2)}) collective-permute-start(f32[8,128]{1,0:T(8,128)S(1)} %decode.1.a), channel_id=1, source_target_pairs={{0,1},{2,3},{1,0},{3,2},{4,5},{6,7},{5,4},{7,6},{8,9},{10,11},{9,8... | collective-permute-start | bytes 12296 | tf_op jit(solution)/shard_map/ppermute | solution.py:329
  46.2 1.0 %copy-start.6 = (bf16[2,2,512,128]{3,2,1,0:T(8,128)(2,1)S(1)}, bf16[2,2,512,128]{3,2,1,0:T(8,128)(2,1)}, u32[]{:S(2)}) copy-start(bf16[2,2,512,128]{3,2,1,0:T(8,128)(2,1)} %get-tuple-element.40.refs_3_) | copy-start | bytes 1572868
  47.2 6.1 %copy-start.8 = (f32[2,16,8,128]{3,2,1,0:T(8,128)S(1)}, f32[2,16,8,128]{3,2,1,0:T(8,128)}, u32[]{:S(2)}) copy-start(f32[2,16,8,128]{3,2,1,0:T(8,128)} %get-tuple-element.46.refs_2_) | copy-start | bytes 393220
  49.9 6.1 %collective-permute-start.1 = (f32[8,128]{1,0:T(8,128)S(1)}, f32[8,128]{1,0:T(8,128)S(1)}, u32[]{:S(2)}, u32[]{:S(2)}) collective-permute-start(f32[8,128]{1,0:T(8,128)S(1)} %add.1.refs_0_), channel_id=1, source_target_pairs={{0,3},{1,2},{3,0},{2,1},{4,7},{5,6},{7,4},{6,5},{8,11},{9,10},{11,... | collective-permute-start | bytes 12296 | tf_op jit(solution)/shard_map/ppermute | solution.py:329
